TPU v7x, 128 devices: a whole 4x4x4 slice. The times are simulated.
128 devices in a mesh: section: 4 (over y_hi, core), dp: 32 (over y_lo, x, z).
Axes of the slice: x: 4, y: 4 (y_hi: 2, y_lo: 2; y = y_hi * 2 + y_lo), z: 4, core: 2. Of those that a mesh axis runs over, the one named last changes fastest.
Arguments:
- entry_states: bfloat16 [5, 1024, 4608], P(None, 'dp'), may hold values from -6 to 6
- down_proj: bfloat16 [4, 4, 4608, 128], P('section'), may hold values from -0.09375 to 0.09375
- up_proj: bfloat16 [4, 4, 4608, 128], P('section'), may hold values from -0.5 to 0.5
- label_rows: bfloat16 [256, 4608], replicated, may hold values from -0.375 to 0.375
- sampled_labels: int32 [4, 5, 1024], P(None, None, 'dp'), may hold values from 0 to 255
- eval_states: bfloat16 [1024, 4608], P('dp'), may hold values from -6 to 6
Outputs:
- eval_out: bfloat16 [4, 1024, 4608], P('section', 'dp')
- label_logprob: float32 [4, 5, 1024], P('section', None, 'dp')
- fisher_log: float32 [4, 2, 4608, 128], P('section', None, 'dp')
All inputs are finite; a program needn't handle non-finite values.
Results may differ from a plain program's by a relative error of at most 0.0065.
Values may be sent and summed in bfloat16 or wider, within the bound.
A program may use at most 128 MiB of HBM per device.

v0:
```python
import jax
import jax.numpy as jnp
from jax import lax
from jax.sharding import PartitionSpec as P

norm_eps = 1e-06
merge_eps = 1e-06
soft_cap = 30.0
gelu_coef = 0.7978845608028654


def from_behind(block, axis, distance):
    devices = range(lax.axis_size(axis))
    route = [(i - distance, i) for i in devices if i - distance in devices]
    return lax.ppermute(block, axis, route)


def in_one_piece(arrays, axis, dim, along):
    both = jnp.concatenate(arrays, axis=along)
    whole, at, outs = (lax.psum_scatter(both, axis, scatter_dimension=dim, tiled=True), 0, [])
    for a in arrays:
        outs.append(lax.slice_in_dim(whole, at, at + a.shape[along], axis=along))
        at += a.shape[along]
    return tuple(outs)


def from_everyone(array, axis):
    peers = lax.axis_size(axis)
    return lax.all_to_all(
        jnp.broadcast_to(array[None], (peers, *array.shape)), axis, 0, 0, tiled=True
    )


def laid_out(pieces, dim):
    pieces = jnp.moveaxis(pieces, 0, dim)
    lengths = pieces.shape
    return pieces.reshape(*lengths[:dim], lengths[dim] * lengths[dim + 1], *lengths[dim + 2 :])


def collect(array, axis, dim):
    pieces = from_everyone(array, axis)
    return laid_out(pieces, dim)


def split_up(array, dim, peers):
    before, after = (array.shape[:dim], array.shape[dim + 1 :])
    return jnp.moveaxis(array.reshape(*before, peers, -1, *after), dim, 0)


def sum_at_owner(array, axis, dim):
    pieces = split_up(array, dim, lax.axis_size(axis))
    arrived = lax.all_to_all(pieces, axis, split_axis=0, concat_axis=0, tiled=True)
    return arrived.sum(axis=0)


def gelu_value(hidden):
    gelu_inner = gelu_coef * (hidden + 0.044715 * hidden * hidden * hidden)
    return 0.5 * hidden * (1.0 + jnp.tanh(gelu_inner))


def gelu_slope(hidden):
    gelu_inner = gelu_coef * (hidden + 0.044715 * hidden * hidden * hidden)
    tanh_value = jnp.tanh(gelu_inner)
    return 0.5 * (1.0 + tanh_value) + 0.5 * hidden * (1.0 - tanh_value * tanh_value) * gelu_coef * (
        1.0 + 3.0 * 0.044715 * hidden * hidden
    )


def block_forward(states, w_down, w_up):
    state_float = states.astype(jnp.float32)
    norm_scale = lax.rsqrt(jnp.mean(state_float * state_float, axis=-1, keepdims=True) + norm_eps)
    norm_float = state_float * norm_scale
    normed = norm_float.astype(jnp.bfloat16)
    hidden = jnp.einsum("tnd,tdr->tnr", normed, w_down, preferred_element_type=jnp.float32)
    active = gelu_value(hidden).astype(jnp.bfloat16)
    update = jnp.einsum("tnr,tdr->tnd", active, w_up, preferred_element_type=jnp.float32)
    output = (state_float + update).astype(jnp.bfloat16)
    return (output, (normed, norm_float, norm_scale, hidden, active))


def label_head(states, labels, label_rows):
    state_float = states.astype(jnp.float32)
    norm_scale = lax.rsqrt(jnp.mean(state_float * state_float, axis=-1, keepdims=True) + norm_eps)
    norm_float = state_float * norm_scale
    normed = norm_float.astype(jnp.bfloat16)
    logits = jnp.einsum("tnd,ld->tnl", normed, label_rows, preferred_element_type=jnp.float32)
    tanh_bent = jnp.tanh(logits / soft_cap)
    capped = soft_cap * tanh_bent
    logprob_all = capped - jnp.log(jnp.sum(jnp.exp(capped), axis=-1, keepdims=True))
    one_hot = (labels[..., None] == lax.broadcasted_iota(jnp.int32, logprob_all.shape, 2)).astype(
        jnp.float32
    )
    picked = jnp.sum(logprob_all * one_hot, axis=-1)
    logit_slope = ((jnp.exp(logprob_all) - one_hot) * (1.0 - tanh_bent * tanh_bent)).astype(
        jnp.bfloat16
    )
    grad_norm = jnp.einsum(
        "tnl,ld->tnd", logit_slope, label_rows, preferred_element_type=jnp.float32
    )
    grad_states = (
        norm_scale
        * (grad_norm - norm_float * jnp.mean(grad_norm * norm_float, axis=-1, keepdims=True))
    ).astype(jnp.bfloat16)
    return (grad_states, picked)


def block_backward(grad_out, saved, w_down, w_up):
    normed, norm_float, norm_scale, hidden, active = saved
    grad_float = grad_out.astype(jnp.float32)
    grad_act = jnp.einsum("tnd,tdr->tnr", grad_out, w_up, preferred_element_type=jnp.float32)
    grad_hidden = (grad_act * gelu_slope(hidden)).astype(jnp.bfloat16)
    grad_norm = jnp.einsum("tnr,tdr->tnd", grad_hidden, w_down, preferred_element_type=jnp.float32)
    grad_in = (
        grad_float
        + norm_scale
        * (grad_norm - norm_float * jnp.mean(grad_norm * norm_float, axis=-1, keepdims=True))
    ).astype(jnp.bfloat16)
    normed_float = normed.astype(jnp.float32)
    hidden_float = grad_hidden.astype(jnp.float32)
    active_float = active.astype(jnp.float32)
    wide_square = jnp.stack([normed_float * normed_float, grad_float * grad_float], axis=1).astype(
        jnp.bfloat16
    )
    narrow_square = jnp.stack(
        [hidden_float * hidden_float, active_float * active_float], axis=1
    ).astype(jnp.bfloat16)
    return (grad_in, wide_square, narrow_square)


def pooled_terms(fisher, stacked):
    numerator = jnp.sum(fisher * stacked.astype(jnp.float32), axis=0)
    denominator = jnp.sum(fisher, axis=0)
    return (numerator, denominator)


def local(entry_states, down_proj, up_proj, label_rows, sampled_labels, eval_states):
    section_count = lax.axis_size("section")
    section_index = lax.axis_index("section")
    last_section = section_count - 1
    w_down = down_proj[0]
    w_up = up_proj[0]
    task_count = w_down.shape[0]
    micro_count = entry_states.shape[0]
    token_rows = entry_states.shape[1]
    model_width = entry_states.shape[2]
    bottleneck = w_down.shape[2]
    turn_count = micro_count + section_count - 1
    state_shape = (task_count, token_rows, model_width)

    def forward_turn(moment, loop_carry):
        incoming, stashed = loop_carry
        micro_index = moment - section_index
        active_turn = (micro_index >= 0) & (micro_index < micro_count)
        clipped = jnp.clip(micro_index, 0, micro_count - 1)
        entry_rows = lax.dynamic_index_in_dim(entry_states, clipped, 0, keepdims=False)
        states = jnp.where(
            section_index == 0, jnp.broadcast_to(entry_rows[None], state_shape), incoming
        )
        output, _ = block_forward(states, w_down, w_up)
        previous = lax.dynamic_index_in_dim(stashed, clipped, 0, keepdims=False)
        stashed = lax.dynamic_update_index_in_dim(
            stashed, jnp.where(active_turn, states, previous), clipped, 0
        )
        incoming = from_behind(output, "section", 1)
        return (incoming, stashed)

    start_states = jnp.zeros(state_shape, jnp.bfloat16)
    start_stash = jnp.zeros((micro_count,) + state_shape, jnp.bfloat16)
    _, stashed = lax.fori_loop(0, turn_count, forward_turn, (start_states, start_stash))

    def backward_turn(moment, loop_carry):
        incoming, wide_all, narrow_all, picked_all = loop_carry
        micro_index = moment - (last_section - section_index)
        active_turn = (micro_index >= 0) & (micro_index < micro_count)
        clipped = jnp.clip(micro_index, 0, micro_count - 1)
        states = lax.dynamic_index_in_dim(stashed, clipped, 0, keepdims=False)
        output, saved = block_forward(states, w_down, w_up)
        labels = lax.dynamic_index_in_dim(sampled_labels, clipped, 1, keepdims=False)
        head_grad, picked = lax.cond(
            section_index == last_section,
            lambda: label_head(output, labels, label_rows),
            lambda: (jnp.zeros(state_shape, jnp.bfloat16), jnp.zeros(labels.shape, jnp.float32)),
        )
        grad_out = jnp.where(section_index == last_section, head_grad, incoming)
        grad_in, wide_square, narrow_square = block_backward(grad_out, saved, w_down, w_up)
        old_wide = lax.dynamic_index_in_dim(wide_all, clipped, 0, keepdims=False)
        wide_all = lax.dynamic_update_index_in_dim(
            wide_all, jnp.where(active_turn, wide_square, old_wide), clipped, 0
        )
        old_narrow = lax.dynamic_index_in_dim(narrow_all, clipped, 0, keepdims=False)
        narrow_all = lax.dynamic_update_index_in_dim(
            narrow_all, jnp.where(active_turn, narrow_square, old_narrow), clipped, 0
        )
        old_picked = lax.dynamic_index_in_dim(picked_all, clipped, 1, keepdims=False)
        picked_all = lax.dynamic_update_index_in_dim(
            picked_all, jnp.where(active_turn, picked, old_picked), clipped, 1
        )
        incoming = from_behind(grad_in, "section", -1)
        return (incoming, wide_all, narrow_all, picked_all)

    start_wide = jnp.zeros((micro_count, task_count, 2, token_rows, model_width), jnp.bfloat16)
    start_narrow = jnp.zeros((micro_count, task_count, 2, token_rows, bottleneck), jnp.bfloat16)
    start_picked = jnp.zeros((task_count, micro_count, token_rows), jnp.float32)
    _, wide_all, narrow_all, picked_all = lax.fori_loop(
        0, turn_count, backward_turn, (start_states, start_wide, start_narrow, start_picked)
    )
    fisher = jnp.einsum(
        "mtknd,mtknr->tkdr", wide_all, narrow_all, preferred_element_type=jnp.float32
    )
    stacked = jnp.stack([w_down, w_up], axis=1)
    numerator, denominator = pooled_terms(fisher, stacked)
    numerator, denominator = in_one_piece((numerator, denominator), "dp", 1, 0)
    merged_part = (numerator / (denominator + merge_eps)).astype(jnp.bfloat16)
    merged = collect(merged_part, "dp", 1)
    fisher_log = jnp.log(denominator + merge_eps)
    merged_down = merged[0][None]
    merged_up = merged[1][None]
    current = eval_states[None]
    result = jnp.zeros_like(eval_states)
    for section_step in range(section_count):
        output, _ = block_forward(current, merged_down, merged_up)
        result = jnp.where(section_index == section_step, output[0], result)
        if section_step + 1 < section_count:
            current = from_behind(output, "section", 1)
    label_logprob = sum_at_owner(picked_all, "section", 0)
    return (result[None], label_logprob, fisher_log[None])


def solution(mesh):
    placed = (
        P(None, "dp", None),
        P("section", None, None, None),
        P("section", None, None, None),
        P(),
        P(None, None, "dp"),
        P("dp", None),
    )
    return jax.shard_map(
        local,
        mesh=mesh,
        in_specs=placed,
        out_specs=(
            P("section", "dp", None),
            P("section", None, "dp"),
            P("section", None, "dp", None),
        ),
        check_vma=False,
    )
```

profile of v0, /device:TPU:17, one launch (start us, length us, event | category | flops | bytes accessed | tf_op | source)
XLA Modules:
  0.0 888.6 jit_solution(15606651125170688822)
XLA Ops:
  7.3 3.1 broadcast_in_dim.93
  10.4 220.2 %while.37 = (s32[]{:T(128)}, bf16[4,32,4608]{2,1,0:T(8,128)(2,1)S(1)}, bf16[5,4,32,4608]{3,2,1,0:T(8,128)(2,1)}, pred[]{:T(512)}, s32[]{:T(128)}, /*index=5*/bf1...) while((s32[]{:T(128)}, ...), condition=%wide.region_3.4_spmd, body=%wide.region_1.3_spmd.sunk | while | flops 310395008 | bytes 27429604 | solution.py:169
  11.8 7.3 fusion.247
  27.0 7.3 fusion.247
  38.3 15.3 %collective-permute-done = bf16[4,32,4608]{2,1,0:T(8,128)(2,1)} collective-permute-done((bf16[4,32,4608]{2,1,0:T(8,128)(2,1)}, bf16[4,32,4608]{2,1,0:T(8,128)(2,1)}, u32[]{:S(2)}, u32[]{:S(2)}) %collective-permute-start) | collective-permute-done | bytes 1179680 | tf_op jit(solution)/shard_map/while/body/eval_jaxpr/ppermute | solution.py:15
  56.3 7.3 fusion.247
  67.6 15.3 %collective-permute-done = bf16[4,32,4608]{2,1,0:T(8,128)(2,1)} collective-permute-done((bf16[4,32,4608]{2,1,0:T(8,128)(2,1)}, bf16[4,32,4608]{2,1,0:T(8,128)(2,1)}, u32[]{:S(2)}, u32[]{:S(2)}) %collective-permute-start) | collective-permute-done | bytes 1179680 | tf_op jit(solution)/shard_map/while/body/eval_jaxpr/ppermute | solution.py:15
  85.6 7.3 fusion.247
  96.9 15.3 %collective-permute-done = bf16[4,32,4608]{2,1,0:T(8,128)(2,1)} collective-permute-done((bf16[4,32,4608]{2,1,0:T(8,128)(2,1)}, bf16[4,32,4608]{2,1,0:T(8,128)(2,1)}, u32[]{:S(2)}, u32[]{:S(2)}) %collective-permute-start) | collective-permute-done | bytes 1179680 | tf_op jit(solution)/shard_map/while/body/eval_jaxpr/ppermute | solution.py:15
  114.9 7.3 fusion.247
  126.2 15.3 %collective-permute-done = bf16[4,32,4608]{2,1,0:T(8,128)(2,1)} collective-permute-done((bf16[4,32,4608]{2,1,0:T(8,128)(2,1)}, bf16[4,32,4608]{2,1,0:T(8,128)(2,1)}, u32[]{:S(2)}, u32[]{:S(2)}) %collective-permute-start) | collective-permute-done | bytes 1179680 | tf_op jit(solution)/shard_map/while/body/eval_jaxpr/ppermute | solution.py:15
  144.2 7.3 fusion.247
  155.5 15.3 %collective-permute-done = bf16[4,32,4608]{2,1,0:T(8,128)(2,1)} collective-permute-done((bf16[4,32,4608]{2,1,0:T(8,128)(2,1)}, bf16[4,32,4608]{2,1,0:T(8,128)(2,1)}, u32[]{:S(2)}, u32[]{:S(2)}) %collective-permute-start) | collective-permute-done | bytes 1179680 | tf_op jit(solution)/shard_map/while/body/eval_jaxpr/ppermute | solution.py:15
  173.5 7.3 fusion.247
  184.8 15.3 %collective-permute-done = bf16[4,32,4608]{2,1,0:T(8,128)(2,1)} collective-permute-done((bf16[4,32,4608]{2,1,0:T(8,128)(2,1)}, bf16[4,32,4608]{2,1,0:T(8,128)(2,1)}, u32[]{:S(2)}, u32[]{:S(2)}) %collective-permute-start) | collective-permute-done | bytes 1179680 | tf_op jit(solution)/shard_map/while/body/eval_jaxpr/ppermute | solution.py:15
  202.7 7.3 fusion.247
  214.1 15.2 %collective-permute-done = bf16[4,32,4608]{2,1,0:T(8,128)(2,1)} collective-permute-done((bf16[4,32,4608]{2,1,0:T(8,128)(2,1)}, bf16[4,32,4608]{2,1,0:T(8,128)(2,1)}, u32[]{:S(2)}, u32[]{:S(2)}) %collective-permute-start) | collective-permute-done | bytes 1179680 | tf_op jit(solution)/shard_map/while/body/eval_jaxpr/ppermute | solution.py:15
  233.1 5.7 broadcast_in_dim.90
  238.8 337.7 %while.38 = (s32[]{:T(128)}, bf16[4,32,4608]{2,1,0:T(8,128)(2,1)}, bf16[5,4,2,32,4608]{4,3,1,2,0:T(8,128)(2,1)}, bf16[5,4,2,32,128]{4,3,1,2,0:T(8,128)(2,1)}, f3...) while((s32[]{:T(128)}, bf16[4,32,4608]{2,1,0:T(8,128)(2,1)}, ...), condition=%wide.region_13.14_spmd, body=%wide.region_4.13_spmd.sunk | while | flops 1243005952 | bytes 103666744 | solution.py:204
  240.6 3.6 fusion.256
  247.2 9.3 %conditional.2 = (bf16[4,32,4608]{2,1,0:T(8,128)(2,1)}, f32[4,32]{1,0:T(4,128)}) conditional(s32[]{:T(128)} %convert_element_type.589, () %tuple.91, (bf16[4,32,4608]{2,1,0:T(8,128)(2,1)S(1)}, bf16[256,4608]{1,0:T(8,128)(2,1)}, s32[4,5,32]{2,0,1:T(4,128)}, s32[]{:T(128)}) %tuple.92), branch_computations={%region_6.6_spmd, %region_7.11_spmd} | conditional | flops 613974784 | bytes 16260656 | solution.py:179
  258.2 3.4 fusion.259
  261.9 3.1 fusion.260
  268.0 9.2 %collective-permute-start.1 = (bf16[4,32,4608]{2,1,0:T(8,128)(2,1)}, bf16[4,32,4608]{2,1,0:T(8,128)(2,1)S(1)}, u32[]{:S(2)}, u32[]{:S(2)}) collective-permute-start(bf16[4,32,4608]{2,1,0:T(8,128)(2,1)} %fusion.261), channel_id=1, source_target_pairs={{32,0},{64,32},{96,64},{33,1},{65,33},{97,65},{34,2},{66,34},{98,6... | collective-permute-start | bytes 3538952 | tf_op jit(solution)/shard_map/while/body/eval_jaxpr/ppermute | solution.py:15
  283.1 3.6 fusion.263
  289.5 3.6 fusion.256
  296.1 9.2 %conditional.2 = (bf16[4,32,4608]{2,1,0:T(8,128)(2,1)}, f32[4,32]{1,0:T(4,128)}) conditional(s32[]{:T(128)} %convert_element_type.589, () %tuple.91, (bf16[4,32,4608]{2,1,0:T(8,128)(2,1)S(1)}, bf16[256,4608]{1,0:T(8,128)(2,1)}, s32[4,5,32]{2,0,1:T(4,128)}, s32[]{:T(128)}) %tuple.92), branch_computations={%region_6.6_spmd, %region_7.11_spmd} | conditional | flops 613974784 | bytes 16260656 | solution.py:179
  307.1 3.4 fusion.259
  324.1 3.7 fusion.263
  330.6 3.6 fusion.256
  337.2 9.3 %conditional.2 = (bf16[4,32,4608]{2,1,0:T(8,128)(2,1)}, f32[4,32]{1,0:T(4,128)}) conditional(s32[]{:T(128)} %convert_element_type.589, () %tuple.91, (bf16[4,32,4608]{2,1,0:T(8,128)(2,1)S(1)}, bf16[256,4608]{1,0:T(8,128)(2,1)}, s32[4,5,32]{2,0,1:T(4,128)}, s32[]{:T(128)}) %tuple.92), branch_computations={%region_6.6_spmd, %region_7.11_spmd} | conditional | flops 613974784 | bytes 16260656 | solution.py:179
  348.2 3.4 fusion.259
  351.9 3.1 fusion.260
  365.3 3.7 fusion.263
  371.8 3.6 fusion.256
  378.4 9.3 %conditional.2 = (bf16[4,32,4608]{2,1,0:T(8,128)(2,1)}, f32[4,32]{1,0:T(4,128)}) conditional(s32[]{:T(128)} %convert_element_type.589, () %tuple.91, (bf16[4,32,4608]{2,1,0:T(8,128)(2,1)S(1)}, bf16[256,4608]{1,0:T(8,128)(2,1)}, s32[4,5,32]{2,0,1:T(4,128)}, s32[]{:T(128)}) %tuple.92), branch_computations={%region_6.6_spmd, %region_7.11_spmd} | conditional | flops 613974784 | bytes 16260656 | solution.py:179
  389.4 3.4 fusion.259
  393.1 3.1 fusion.260
  406.5 3.6 fusion.263
  412.9 3.6 fusion.256
  419.5 9.3 %conditional.2 = (bf16[4,32,4608]{2,1,0:T(8,128)(2,1)}, f32[4,32]{1,0:T(4,128)}) conditional(s32[]{:T(128)} %convert_element_type.589, () %tuple.91, (bf16[4,32,4608]{2,1,0:T(8,128)(2,1)S(1)}, bf16[256,4608]{1,0:T(8,128)(2,1)}, s32[4,5,32]{2,0,1:T(4,128)}, s32[]{:T(128)}) %tuple.92), branch_computations={%region_6.6_spmd, %region_7.11_spmd} | conditional | flops 613974784 | bytes 16260656 | solution.py:179
  430.5 3.4 fusion.259
  447.6 3.7 fusion.263
  454.1 3.6 fusion.256
  460.8 9.2 %conditional.2 = (bf16[4,32,4608]{2,1,0:T(8,128)(2,1)}, f32[4,32]{1,0:T(4,128)}) conditional(s32[]{:T(128)} %convert_element_type.589, () %tuple.91, (bf16[4,32,4608]{2,1,0:T(8,128)(2,1)S(1)}, bf16[256,4608]{1,0:T(8,128)(2,1)}, s32[4,5,32]{2,0,1:T(4,128)}, s32[]{:T(128)}) %tuple.92), branch_computations={%region_6.6_spmd, %region_7.11_spmd} | conditional | flops 613974784 | bytes 16260656 | solution.py:179
  471.7 3.4 fusion.259
  488.2 3.7 fusion.263
  494.7 3.6 fusion.256
  501.3 9.3 %conditional.2 = (bf16[4,32,4608]{2,1,0:T(8,128)(2,1)}, f32[4,32]{1,0:T(4,128)}) conditional(s32[]{:T(128)} %convert_element_type.589, () %tuple.91, (bf16[4,32,4608]{2,1,0:T(8,128)(2,1)S(1)}, bf16[256,4608]{1,0:T(8,128)(2,1)}, s32[4,5,32]{2,0,1:T(4,128)}, s32[]{:T(128)}) %tuple.92), branch_computations={%region_6.6_spmd, %region_7.11_spmd} | conditional | flops 613974784 | bytes 16260656 | solution.py:179
  512.3 3.4 fusion.259
  530.0 3.7 fusion.263
  536.5 3.6 fusion.256
  543.1 9.3 %conditional.2 = (bf16[4,32,4608]{2,1,0:T(8,128)(2,1)}, f32[4,32]{1,0:T(4,128)}) conditional(s32[]{:T(128)} %convert_element_type.589, () %tuple.91, (bf16[4,32,4608]{2,1,0:T(8,128)(2,1)S(1)}, bf16[256,4608]{1,0:T(8,128)(2,1)}, s32[4,5,32]{2,0,1:T(4,128)}, s32[]{:T(128)}) %tuple.92), branch_computations={%region_6.6_spmd, %region_7.11_spmd} | conditional | flops 613974784 | bytes 16260656 | solution.py:179
  554.1 3.4 fusion.259
  571.8 3.7 fusion.263
  576.6 12.8 %fusion.201 = f32[4,2,4608,128,1]{3,2,0,1,4:T(8,128)} fusion(bf16[5,4,2,32,4608]{4,3,1,2,0:T(8,128)(2,1)} %get-tuple-element.447, bf16[5,4,2,32,128]{4,3,1,2,0:T(8,128)(2,1)} %get-tuple-element.448), kind=kOutput, calls=%fused_computation.227 | convolution fusion | flops 1509949440 | bytes 30998528 | tf_op jit(solution)/shard_map/mtknd,mtknr->tkdr/dot_general | solution.py:207
  589.4 14.0 %fusion.96 = (f32[2,4608,128]{2,1,0:T(8,128)}, f32[2,4608,128]{2,1,0:T(8,128)}) fusion(f32[4,2,4608,128,1]{3,2,0,1,4:T(8,128)} %fusion.201, bf16[4,1,4608,128]{3,2,1,0:T(8,128)(2,1)S(1)} %bitcast.209, bf16[4,1,4608,128]{3,2,1,0:T(8,128)(2,1)S(1)} %bitcast.203), kind=kLoop, calls=%fused_computation.117 | loop fusion | flops 21233664 | bytes 37748736 | tf_op jit(solution)/shard_map/reduce_sum | solution.py:131
  603.5 8.0 pad_maximum_fusion
  611.5 170.8 %reduce-scatter.2.cloned.1.call-done = f32[4,144,128]{2,1,0:T(8,128)} async-done(((f32[4,4608,128]{2,1,0:T(8,128)}), f32[4,144,128]{2,1,0:T(8,128)}) %reduce-scatter.2.cloned.1.call-update) | async-done | bytes 294928 | tf_op jit(solution)/shard_map/reduce_scatter | solution.py:20
  785.7 4.2 all-to-all-start
  790.1 19.4 %all-to-all-done = bf16[32,2,144,128]{3,2,1,0:T(8,128)(2,1)S(1)} async-done(((bf16[32,2,144,128]{3,2,1,0:T(8,128)(2,1)}), bf16[32,2,144,128]{3,2,1,0:T(8,128)(2,1)S(1)}, u32[]{:S(2)}, u32[]{:S(2)}) %all-to-all-start) | async-done | bytes 2359328 | tf_op jit(solution)/shard_map/all_to_all | solution.py:29
  814.9 32.8 %collective-permute-done.2 = bf16[1,32,4608]{2,1,0:T(8,128)(2,1)S(1)} collective-permute-done((bf16[1,32,4608]{2,1,0:T(8,128)(2,1)S(1)}, bf16[1,32,4608]{2,1,0:T(8,128)(2,1)S(1)}, u32[]{:S(2)}, u32[]{:S(2)}) %collective-permute-start.2) | collective-permute-done | bytes 294944 | tf_op jit(solution)/shard_map/ppermute | solution.py:15
  850.2 8.2 collective-permute-done.3
  863.9 11.7 %all-to-all-start.1 = ((f32[4,1,160]{2,1,0:T(1,128)}), f32[4,1,160]{2,1,0:T(1,128)S(1)}, u32[]{:S(2)}, u32[]{:S(2)}) async-start(f32[4,1,160]{2,1,0:T(1,128)} %reshape.327), calls=%async_computation.2 | async-start | bytes 8192 | tf_op jit(solution)/shard_map/all_to_all | solution.py:52
  (439 shorter events, 313.3 us)
Async XLA Ops:
  7.2 775.2 %reduce-scatter.2.cloned.1.call-start = ((), (), s32[]{:S(2)}) async-start(), calls=%async_computation.3 | async-start | bytes 9732096 | tf_op jit(solution)/shard_map/reduce_scatter | solution.py:20
  19.1 5.2 collective-permute-start
  34.3 19.3 %collective-permute-start = (bf16[4,32,4608]{2,1,0:T(8,128)(2,1)}, bf16[4,32,4608]{2,1,0:T(8,128)(2,1)}, u32[]{:S(2)}, u32[]{:S(2)}) collective-permute-start(bf16[4,32,4608]{2,1,0:T(8,128)(2,1)} %fusion.247), channel_id=1, source_target_pairs={{0,32},{32,64},{64,96},{1,33},{33,65},{65,97},{2,34},{34,66},{66,9... | collective-permute-start | bytes 3538952 | tf_op jit(solution)/shard_map/while/body/eval_jaxpr/ppermute | solution.py:15
  63.6 19.3 %collective-permute-start = (bf16[4,32,4608]{2,1,0:T(8,128)(2,1)}, bf16[4,32,4608]{2,1,0:T(8,128)(2,1)}, u32[]{:S(2)}, u32[]{:S(2)}) collective-permute-start(bf16[4,32,4608]{2,1,0:T(8,128)(2,1)} %fusion.247), channel_id=1, source_target_pairs={{0,32},{32,64},{64,96},{1,33},{33,65},{65,97},{2,34},{34,66},{66,9... | collective-permute-start | bytes 3538952 | tf_op jit(solution)/shard_map/while/body/eval_jaxpr/ppermute | solution.py:15
  92.9 19.3 %collective-permute-start = (bf16[4,32,4608]{2,1,0:T(8,128)(2,1)}, bf16[4,32,4608]{2,1,0:T(8,128)(2,1)}, u32[]{:S(2)}, u32[]{:S(2)}) collective-permute-start(bf16[4,32,4608]{2,1,0:T(8,128)(2,1)} %fusion.247), channel_id=1, source_target_pairs={{0,32},{32,64},{64,96},{1,33},{33,65},{65,97},{2,34},{34,66},{66,9... | collective-permute-start | bytes 3538952 | tf_op jit(solution)/shard_map/while/body/eval_jaxpr/ppermute | solution.py:15
  122.2 19.3 %collective-permute-start = (bf16[4,32,4608]{2,1,0:T(8,128)(2,1)}, bf16[4,32,4608]{2,1,0:T(8,128)(2,1)}, u32[]{:S(2)}, u32[]{:S(2)}) collective-permute-start(bf16[4,32,4608]{2,1,0:T(8,128)(2,1)} %fusion.247), channel_id=1, source_target_pairs={{0,32},{32,64},{64,96},{1,33},{33,65},{65,97},{2,34},{34,66},{66,9... | collective-permute-start | bytes 3538952 | tf_op jit(solution)/shard_map/while/body/eval_jaxpr/ppermute | solution.py:15
  151.4 19.3 %collective-permute-start = (bf16[4,32,4608]{2,1,0:T(8,128)(2,1)}, bf16[4,32,4608]{2,1,0:T(8,128)(2,1)}, u32[]{:S(2)}, u32[]{:S(2)}) collective-permute-start(bf16[4,32,4608]{2,1,0:T(8,128)(2,1)} %fusion.247), channel_id=1, source_target_pairs={{0,32},{32,64},{64,96},{1,33},{33,65},{65,97},{2,34},{34,66},{66,9... | collective-permute-start | bytes 3538952 | tf_op jit(solution)/shard_map/while/body/eval_jaxpr/ppermute | solution.py:15
  180.7 19.3 %collective-permute-start = (bf16[4,32,4608]{2,1,0:T(8,128)(2,1)}, bf16[4,32,4608]{2,1,0:T(8,128)(2,1)}, u32[]{:S(2)}, u32[]{:S(2)}) collective-permute-start(bf16[4,32,4608]{2,1,0:T(8,128)(2,1)} %fusion.247), channel_id=1, source_target_pairs={{0,32},{32,64},{64,96},{1,33},{33,65},{65,97},{2,34},{34,66},{66,9... | collective-permute-start | bytes 3538952 | tf_op jit(solution)/shard_map/while/body/eval_jaxpr/ppermute | solution.py:15
  210.0 19.3 %collective-permute-start = (bf16[4,32,4608]{2,1,0:T(8,128)(2,1)}, bf16[4,32,4608]{2,1,0:T(8,128)(2,1)}, u32[]{:S(2)}, u32[]{:S(2)}) collective-permute-start(bf16[4,32,4608]{2,1,0:T(8,128)(2,1)} %fusion.247), channel_id=1, source_target_pairs={{0,32},{32,64},{64,96},{1,33},{33,65},{65,97},{2,34},{34,66},{66,9... | collective-permute-start | bytes 3538952 | tf_op jit(solution)/shard_map/while/body/eval_jaxpr/ppermute | solution.py:15
  238.8 5.4 slice-start.4
  240.6 3.6 slice-start.5
  258.2 3.6 slice-start
  258.2 3.7 slice-start.1
  261.9 3.1 copy-start.3
  268.0 18.7 %collective-permute-start.1 = (bf16[4,32,4608]{2,1,0:T(8,128)(2,1)}, bf16[4,32,4608]{2,1,0:T(8,128)(2,1)S(1)}, u32[]{:S(2)}, u32[]{:S(2)}) collective-permute-start(bf16[4,32,4608]{2,1,0:T(8,128)(2,1)} %fusion.261), channel_id=1, source_target_pairs={{32,0},{64,32},{96,64},{33,1},{65,33},{97,65},{34,2},{66,34},{98,6... | collective-permute-start | bytes 3538952 | tf_op jit(solution)/shard_map/while/body/eval_jaxpr/ppermute | solution.py:15
  287.7 5.4 slice-start.4
  289.5 3.6 slice-start.5
  307.0 3.6 slice-start
  307.1 3.7 slice-start.1
  316.8 11.0 %collective-permute-start.1 = (bf16[4,32,4608]{2,1,0:T(8,128)(2,1)}, bf16[4,32,4608]{2,1,0:T(8,128)(2,1)S(1)}, u32[]{:S(2)}, u32[]{:S(2)}) collective-permute-start(bf16[4,32,4608]{2,1,0:T(8,128)(2,1)} %fusion.261), channel_id=1, source_target_pairs={{32,0},{64,32},{96,64},{33,1},{65,33},{97,65},{34,2},{66,34},{98,6... | collective-permute-start | bytes 3538952 | tf_op jit(solution)/shard_map/while/body/eval_jaxpr/ppermute | solution.py:15
  328.8 5.4 slice-start.4
  330.6 3.6 slice-start.5
  348.2 3.6 slice-start
  348.2 3.7 slice-start.1
  358.0 11.0 %collective-permute-start.1 = (bf16[4,32,4608]{2,1,0:T(8,128)(2,1)}, bf16[4,32,4608]{2,1,0:T(8,128)(2,1)S(1)}, u32[]{:S(2)}, u32[]{:S(2)}) collective-permute-start(bf16[4,32,4608]{2,1,0:T(8,128)(2,1)} %fusion.261), channel_id=1, source_target_pairs={{32,0},{64,32},{96,64},{33,1},{65,33},{97,65},{34,2},{66,34},{98,6... | collective-permute-start | bytes 3538952 | tf_op jit(solution)/shard_map/while/body/eval_jaxpr/ppermute | solution.py:15
  370.0 5.4 slice-start.4
  371.8 3.6 slice-start.5
  389.3 3.6 slice-start
  389.4 3.7 slice-start.1
  393.1 3.1 copy-start.3
  399.1 11.0 %collective-permute-start.1 = (bf16[4,32,4608]{2,1,0:T(8,128)(2,1)}, bf16[4,32,4608]{2,1,0:T(8,128)(2,1)S(1)}, u32[]{:S(2)}, u32[]{:S(2)}) collective-permute-start(bf16[4,32,4608]{2,1,0:T(8,128)(2,1)} %fusion.261), channel_id=1, source_target_pairs={{32,0},{64,32},{96,64},{33,1},{65,33},{97,65},{34,2},{66,34},{98,6... | collective-permute-start | bytes 3538952 | tf_op jit(solution)/shard_map/while/body/eval_jaxpr/ppermute | solution.py:15
  411.1 5.4 slice-start.4
  412.9 3.6 slice-start.5
  430.5 3.6 slice-start
  430.5 3.7 slice-start.1
  434.2 3.1 copy-start.3
  440.3 11.1 %collective-permute-start.1 = (bf16[4,32,4608]{2,1,0:T(8,128)(2,1)}, bf16[4,32,4608]{2,1,0:T(8,128)(2,1)S(1)}, u32[]{:S(2)}, u32[]{:S(2)}) collective-permute-start(bf16[4,32,4608]{2,1,0:T(8,128)(2,1)} %fusion.261), channel_id=1, source_target_pairs={{32,0},{64,32},{96,64},{33,1},{65,33},{97,65},{34,2},{66,34},{98,6... | collective-permute-start | bytes 3538952 | tf_op jit(solution)/shard_map/while/body/eval_jaxpr/ppermute | solution.py:15
  452.4 5.4 slice-start.4
  454.1 3.6 slice-start.5
  471.7 3.6 slice-start
  471.7 3.7 slice-start.1
  481.5 10.4 %collective-permute-start.1 = (bf16[4,32,4608]{2,1,0:T(8,128)(2,1)}, bf16[4,32,4608]{2,1,0:T(8,128)(2,1)S(1)}, u32[]{:S(2)}, u32[]{:S(2)}) collective-permute-start(bf16[4,32,4608]{2,1,0:T(8,128)(2,1)} %fusion.261), channel_id=1, source_target_pairs={{32,0},{64,32},{96,64},{33,1},{65,33},{97,65},{34,2},{66,34},{98,6... | collective-permute-start | bytes 3538952 | tf_op jit(solution)/shard_map/while/body/eval_jaxpr/ppermute | solution.py:15
  492.9 5.4 slice-start.4
  494.7 3.6 slice-start.5
  512.3 3.6 slice-start
  512.3 3.7 slice-start.1
  516.0 3.1 copy-start.3
  522.1 11.7 %collective-permute-start.1 = (bf16[4,32,4608]{2,1,0:T(8,128)(2,1)}, bf16[4,32,4608]{2,1,0:T(8,128)(2,1)S(1)}, u32[]{:S(2)}, u32[]{:S(2)}) collective-permute-start(bf16[4,32,4608]{2,1,0:T(8,128)(2,1)} %fusion.261), channel_id=1, source_target_pairs={{32,0},{64,32},{96,64},{33,1},{65,33},{97,65},{34,2},{66,34},{98,6... | collective-permute-start | bytes 3538952 | tf_op jit(solution)/shard_map/while/body/eval_jaxpr/ppermute | solution.py:15
  534.7 5.4 slice-start.4
  536.5 3.6 slice-start.5
  554.1 3.6 slice-start
  554.1 3.7 slice-start.1
  563.9 11.7 %collective-permute-start.1 = (bf16[4,32,4608]{2,1,0:T(8,128)(2,1)}, bf16[4,32,4608]{2,1,0:T(8,128)(2,1)S(1)}, u32[]{:S(2)}, u32[]{:S(2)}) collective-permute-start(bf16[4,32,4608]{2,1,0:T(8,128)(2,1)} %fusion.261), channel_id=1, source_target_pairs={{32,0},{64,32},{96,64},{33,1},{65,33},{97,65},{34,2},{66,34},{98,6... | collective-permute-start | bytes 3538952 | tf_op jit(solution)/shard_map/while/body/eval_jaxpr/ppermute | solution.py:15
  576.6 12.8 %slice-start.2 = ((s8[4718592]{0:T(1024)(128)(4,1)}), s8[4194304]{0:T(1024)(128)(4,1)S(1)}, s32[]{:S(2)}) async-start(s8[4718592]{0:T(1024)(128)(4,1)} %bitcast.201), calls=%async_computation.6 | async-start | bytes 8388608
  576.6 12.8 %slice-start.6 = ((s8[4718592]{0:T(1024)(128)(4,1)}), s8[4194304]{0:T(1024)(128)(4,1)S(1)}, s32[]{:S(2)}) async-start(s8[4718592]{0:T(1024)(128)(4,1)} %bitcast.207), calls=%async_computation.10 | async-start | bytes 8388608
  576.6 12.8 %slice-start.3 = ((s8[4718592]{0:T(1024)(128)(4,1)}), s8[524288]{0:T(1024)(128)(4,1)S(1)}, s32[]{:S(2)}) async-start(s8[4718592]{0:T(1024)(128)(4,1)} %bitcast.201), calls=%async_computation.7 | async-start | bytes 1048576
  576.6 12.8 %slice-start.7 = ((s8[4718592]{0:T(1024)(128)(4,1)}), s8[524288]{0:T(1024)(128)(4,1)S(1)}, s32[]{:S(2)}) async-start(s8[4718592]{0:T(1024)(128)(4,1)} %bitcast.207), calls=%async_computation.11 | async-start | bytes 1048576
  785.7 4.2 copy-start.5
  785.7 23.8 %all-to-all-start = ((bf16[32,2,144,128]{3,2,1,0:T(8,128)(2,1)}), bf16[32,2,144,128]{3,2,1,0:T(8,128)(2,1)S(1)}, u32[]{:S(2)}, u32[]{:S(2)}) async-start(bf16[32,2,144,128]{3,2,1,0:T(8,128)(2,1)} %broadcast_in_dim.94), calls=%async_computation.1 | async-start | bytes 4718592 | tf_op jit(solution)/shard_map/all_to_all | solution.py:29
  813.6 34.1 %collective-permute-start.2 = (bf16[1,32,4608]{2,1,0:T(8,128)(2,1)S(1)}, bf16[1,32,4608]{2,1,0:T(8,128)(2,1)S(1)}, u32[]{:S(2)}, u32[]{:S(2)}) collective-permute-start(bf16[1,32,4608]{2,1,0:T(8,128)(2,1)S(1)} %bitcast.219), channel_id=1, source_target_pairs={{0,32},{32,64},{64,96},{1,33},{33,65},{65,97},{2,34},{34,66},{66,9... | collective-permute-start | bytes 884744 | tf_op jit(solution)/shard_map/ppermute | solution.py:15
  848.7 12.0 %copy-start.7 = (f32[4,5,32]{2,0,1:T(4,128)S(1)}, f32[4,5,32]{2,0,1:T(4,128)}, u32[]{:S(2)}) copy-start(f32[4,5,32]{2,0,1:T(4,128)} %get-tuple-element.449) | copy-start | bytes 7684
  848.7 9.7 %collective-permute-start.3 = (bf16[1,32,4608]{2,1,0:T(8,128)(2,1)S(1)}, bf16[1,32,4608]{2,1,0:T(8,128)(2,1)S(1)}, u32[]{:S(2)}, u32[]{:S(2)}) collective-permute-start(bf16[1,32,4608]{2,1,0:T(8,128)(2,1)S(1)} %fusion.100), channel_id=1, source_target_pairs={{0,32},{32,64},{64,96},{1,33},{33,65},{65,97},{2,34},{34,66},{66,9... | collective-permute-start | bytes 884744 | tf_op jit(solution)/shard_map/ppermute | solution.py:15
  859.4 20.6 %collective-permute-start.4 = (bf16[1,32,4608]{2,1,0:T(8,128)(2,1)S(1)}, bf16[1,32,4608]{2,1,0:T(8,128)(2,1)S(1)}, u32[]{:S(2)}, u32[]{:S(2)}) collective-permute-start(bf16[1,32,4608]{2,1,0:T(8,128)(2,1)S(1)} %fusion.101), channel_id=1, source_target_pairs={{0,32},{32,64},{64,96},{1,33},{33,65},{65,97},{2,34},{34,66},{66,9... | collective-permute-start | bytes 884744 | tf_op jit(solution)/shard_map/ppermute | solution.py:15
  863.9 14.7 %all-to-all-start.1 = ((f32[4,1,160]{2,1,0:T(1,128)}), f32[4,1,160]{2,1,0:T(1,128)S(1)}, u32[]{:S(2)}, u32[]{:S(2)}) async-start(f32[4,1,160]{2,1,0:T(1,128)} %reshape.327), calls=%async_computation.2 | async-start | bytes 8192 | tf_op jit(solution)/shard_map/all_to_all | solution.py:52
  (37 other events, 65.3 us)
Sparse Core Ops, SparseCore 0:
  611.6 170.6 reduce-scatter.1
where the time goes:
time: 896 us; the launch traced here: 889 us
  waiting for transfers between devices  343 us (38%)
  matrix products  220 us (25%)
  other arithmetic  184 us (21%)
  local copies, waits for them, and re-layouts  74.8 us (8%)
  starting transfers between devices  51.3 us (6%)
  between operations  14.2 us (2%)
    reduce_scatter x1, waiting for transfers between devices, in_one_piece(): lax.psum_scatter(both, axis, scatter_dimension=dim, tiled=True)  171 us
    ppermute x19, waiting for transfers between devices, from_behind(): return lax.ppermute(block, axis, route)  149 us
    dot_general x20, matrix products, block_forward(): jnp.einsum('tnr,tdr->tnd', active, w_up, preferred_element_type=jnp.float32)  86.2 us
    ppermute x19, starting transfers between devices, from_behind(): return lax.ppermute(block, axis, route)  35.4 us
    dynamic_update_slice x8, other arithmetic, backward_turn(): lax.dynamic_update_index_in_dim(wide_all, jnp.where(active_turn, wide_squ...  29.6 us
    dot_general x8, matrix products, block_forward(): jnp.einsum('tnd,tdr->tnr', normed, w_down, preferred_element_type=jnp.flo...  28.6 us
    dot_general x8, matrix products, block_backward(): jnp.einsum('tnd,tdr->tnr', grad_out, w_up, preferred_element_type=jnp.flo...  26.9 us
    another operation x16, other arithmetic, block_backward(): jnp.stack([normed_float * normed_float, grad_float * grad_float], axis=1)  26.4 us
  transfers between devices with their start and end apart: 22, of which 13 were waited for; matrix products, arithmetic and copies ran while one was open for 11% of the time, Pallas kernels for 0%

commit v1 on v0

v1 whole, which is shorter than its diff:
```python
import jax
import jax.numpy as jnp
from jax import lax
from jax.experimental import pallas as pl
from jax.experimental.pallas import tpu as pltpu
from jax.sharding import PartitionSpec as P

norm_eps = 1e-06
merge_eps = 1e-06
soft_cap = 30.0
gelu_coef = 0.7978845608028654

D = 4608
R = 128
LABELS = 256
TASKS = 4
MICRO = 5
ROWS = 32
N = MICRO * ROWS
TILE = 512
BLK = D // 4
F32 = jnp.float32
BF16 = jnp.bfloat16
MESH = pl.DeviceIdType.MESH


def gelu_value(hidden):
    inner = gelu_coef * (hidden + 0.044715 * hidden * hidden * hidden)
    return 0.5 * hidden * (1.0 + jnp.tanh(inner))


def gelu_slope(hidden):
    inner = gelu_coef * (hidden + 0.044715 * hidden * hidden * hidden)
    t = jnp.tanh(inner)
    return 0.5 * (1.0 + t) + 0.5 * hidden * (1.0 - t * t) * gelu_coef * (
        1.0 + 3.0 * 0.044715 * hidden * hidden
    )


def dot_nn(a, b):
    return lax.dot_general(a, b, (((1,), (0,)), ((), ())), preferred_element_type=F32)


def dot_nt(a, b):
    return lax.dot_general(a, b, (((1,), (1,)), ((), ())), preferred_element_type=F32)


def dot_tn(a, b):
    return lax.dot_general(a, b, (((0,), (0,)), ((), ())), preferred_element_type=F32)


def lane_fold(v):
    total = v[:, 0:128]
    for i in range(1, v.shape[1] // 128):
        total = total + v[:, i * 128 : (i + 1) * 128]
    return total


def kernel(
    down, up, entry, labels, label_rows, evals,
    eval_out, logp_out, flog_out,
    w, x, g, rows, lab, n2, g2, hid, act, scale,
    fb, r1, r2, s2, r3, s3, r4, wd, merged, vin, picked,
    load_sem, ps, pr, cs, cr, as_, ar, bs, br, os_, orr, es, er, fs, fr,
    s1s, s1r, s2s, s2r, ys, yr, gs, gr, vs, vr,
):
    s = lax.axis_index("section")
    d = lax.axis_index("dp")
    h = s // 2
    c = s % 2
    yl = d // 16
    xx = (d // 4) % 4
    zz = d % 4
    y = 2 * h + yl
    u = xx * (1 - c) + zz * c
    v = zz * (1 - c) + xx * c

    def at(h_, c_, yl_, x_, z_):
        return {"section": h_ * 2 + c_, "dp": yl_ * 16 + x_ * 4 + z_}

    def at_uv(u_, v_):
        return at(h, c, yl, u_ * (1 - c) + v_ * c, v_ * (1 - c) + u_ * c)

    def at_y(y_):
        return at(y_ // 2, c, y_ % 2, xx, zz)

    partner = at(h, 1 - c, yl, xx, zz)
    swap = at(h, 1 - c, 1 - yl, xx, zz)
    across = at(1 - h, c, 1 - yl, xx, zz)
    after = at(1 - h, 1 - c, yl, xx, zz)
    a_peers = [None] + [at_uv((u + i) % 4, v) for i in range(1, 4)]
    b_peers = [None] + [at_uv(u, (v + i) % 4) for i in range(1, 4)]
    y_peers = [None] + [at_y((y + i) % 4) for i in range(1, 4)]

    def remote(src, dst, send, recv, to):
        return pltpu.make_async_remote_copy(
            src_ref=src, dst_ref=dst, send_sem=send, recv_sem=recv, device_id=to, device_id_type=MESH
        )

    barrier = pltpu.get_barrier_semaphore()
    everyone = [partner, swap, after] + a_peers[1:] + b_peers[1:] + y_peers[1:]
    for peer in everyone:
        pl.semaphore_signal(barrier, inc=1, device_id=peer, device_id_type=MESH)
    pl.semaphore_wait(barrier, len(everyone))

    far = 3 - y
    own = u * 4 + v
    part = D // 16
    slice_rows = pl.ds(own * part, part)
    cross = [
        remote(down.at[far, slice_rows], w.at[s, 0, slice_rows], cs.at[0], cr.at[0], across),
        remote(up.at[far, slice_rows], w.at[s, 1, slice_rows], cs.at[1], cr.at[1], across),
    ]
    for copy in cross:
        copy.start()
    beside = [
        remote(down.at[y], w.at[s, 0], ps.at[0], pr.at[0], partner),
        remote(up.at[y], w.at[s, 1], ps.at[1], pr.at[1], partner),
    ]
    moved = [
        remote(entry, x.at[0], es.at[0], er.at[0], swap),
        remote(labels.at[2 * h + 1 - yl], lab, es.at[1], er.at[1], swap),
    ]
    kept = [
        pltpu.make_async_copy(entry, x.at[0], load_sem.at[0]),
        pltpu.make_async_copy(labels.at[y], lab, load_sem.at[1]),
    ]

    @pl.when(c != yl)
    def _():
        for copy in moved:
            copy.start()

    @pl.when(c == yl)
    def _():
        for copy in kept:
            copy.start()

    for copy in beside:
        copy.start()
    loads = [
        pltpu.make_async_copy(down.at[y], w.at[s, 0], load_sem.at[2]),
        pltpu.make_async_copy(up.at[y], w.at[s, 1], load_sem.at[3]),
        pltpu.make_async_copy(label_rows, rows, load_sem.at[4]),
    ]
    mine = pl.ds(pl.multiple_of(d * 144, 16), 144)
    for t in range(TASKS):
        loads.append(pltpu.make_async_copy(down.at[t, mine], wd.at[t, 0], load_sem.at[5 + 2 * t]))
        loads.append(pltpu.make_async_copy(up.at[t, mine], wd.at[t, 1], load_sem.at[6 + 2 * t]))
    for copy in loads:
        copy.start()
    eval_load = pltpu.make_async_copy(evals, vin, load_sem.at[13])

    @pl.when(s == 0)
    def _():
        eval_load.start()

    lr = 2 * (1 - h) + c

    def piece(u_, v_):
        return w.at[lr, :, pl.ds((u_ * 4 + v_) * part, part)]

    for copy in cross:
        copy.wait_recv()
    a_sends = []
    for i in range(1, 4):
        copy = remote(piece(u, v), piece(u, v), as_.at[i], ar.at[i], a_peers[i])
        copy.start()
        a_sends.append(copy)
    b_sends = []
    for i in range(4):
        if i:
            from_u = (u + 4 - i) % 4
            remote(piece(from_u, v), piece(from_u, v), as_.at[i], ar.at[i], a_peers[i]).wait_recv()
        else:
            from_u = u
        for j in range(1, 4):
            copy = remote(piece(from_u, v), piece(from_u, v), bs.at[i, j], br.at[i, j], b_peers[j])
            copy.start()
            b_sends.append(copy)
    o_sends = []
    for i in range(4):
        from_u = (u + 4 - i) % 4
        for j in range(1, 4):
            from_v = (v + 4 - j) % 4
            remote(piece(from_u, from_v), piece(from_u, from_v), bs.at[i, j], br.at[i, j], b_peers[j]).wait_recv()
        block = w.at[lr, :, pl.ds(from_u * BLK, BLK)]
        copy = remote(block, block, os_.at[i], orr.at[i], partner)
        copy.start()
        o_sends.append(copy)

    @pl.when(c != yl)
    def _():
        for copy in moved:
            copy.wait()

    @pl.when(c == yl)
    def _():
        for copy in kept:
            copy.wait()

    for copy in beside:
        copy.wait()
    for copy in loads:
        copy.wait()
    for copy in cross + a_sends + b_sends:
        copy.wait_send()
    for copy in o_sends:
        copy.wait()

    zero = jnp.zeros((N, 128), F32)

    def cols(f, size=TILE):
        return pl.ds(pl.multiple_of(f * size, size), size)

    def first(f, carry):
        total, acc = carry
        xt = x[0, :, cols(f)]
        xf = xt.astype(F32)
        return total + lane_fold(xf * xf), acc + dot_nn(xt, w[0, 0, cols(f), :])

    total, acc = lax.fori_loop(0, D // TILE, first, (zero, zero))
    for k in range(4):
        sk = lax.rsqrt(jnp.sum(total, axis=1, keepdims=True) * (1.0 / D) + norm_eps)
        hk = sk * acc
        scale[k] = jnp.broadcast_to(sk, (N, 128))
        hid[k] = hk
        ak = gelu_value(hk).astype(BF16)
        act[k] = ak

        def step(f, carry, k=k, ak=ak):
            total, acc = carry
            new = (x[k, :, cols(f)].astype(F32) + dot_nt(ak, w[k, 1, cols(f), :])).astype(BF16)
            x[k + 1, :, cols(f)] = new
            nf = new.astype(F32)
            if k < 3:
                more = dot_nn(new, w[k + 1, 0, cols(f), :])
            else:
                more = dot_nt(new, rows[:, cols(f)])
            return total + lane_fold(nf * nf), acc + more

        width = R if k < 3 else LABELS
        total, acc = lax.fori_loop(0, D // TILE, step, (zero, jnp.zeros((N, width), F32)))

    sy = lax.rsqrt(jnp.sum(total, axis=1, keepdims=True) * (1.0 / D) + norm_eps)
    logits = sy * acc
    bent = jnp.tanh(logits * (1.0 / soft_cap))
    capped = soft_cap * bent
    logp = capped - jnp.log(jnp.sum(jnp.exp(capped), axis=1, keepdims=True))
    hot = lab[:, 0:1] == lax.broadcasted_iota(jnp.int32, (N, LABELS), 1)
    chosen = jnp.sum(jnp.where(hot, logp, 0.0), axis=1, keepdims=True)
    picked[...] = jnp.broadcast_to(chosen, (N, 128))
    give = remote(picked, logp_out, es.at[2], er.at[2], swap)
    hold = pltpu.make_async_copy(picked, logp_out, load_sem.at[14])

    @pl.when(c != yl)
    def _():
        give.start()

    @pl.when(c == yl)
    def _():
        hold.start()

    e = ((jnp.exp(logp) - jnp.where(hot, 1.0, 0.0)) * (1.0 - bent * bent)).astype(BF16)
    mean = jnp.sum(e.astype(F32) * logits, axis=1, keepdims=True) * (1.0 / D)
    sm = sy * mean

    def head(f, acc):
        back = dot_nn(e, rows[:, cols(f)])
        gy = (sy * (back - x[4, :, cols(f)].astype(F32) * sm)).astype(BF16)
        g[:, cols(f)] = gy
        return acc + dot_nn(gy, w[3, 1, cols(f), :])

    ga = lax.fori_loop(0, D // TILE, head, zero)

    def keep_or_send(k):
        return remote(fb.at[k], r1.at[k // 2], fs.at[k // 2], fr.at[k // 2], partner)

    def source(hh, q):
        return fb.at[2 * hh + c, :, :, q], fb.at[2 * hh + c, :, :, :, q]

    def stage_one(hh, i, view):
        return remote(view, r2.at[hh, i - 1], s1s.at[hh, i], s1r.at[hh, i], a_peers[i])

    def open_sum(hh):
        k = 2 * hh + c
        remote(fb.at[k], r1.at[hh], fs.at[hh], fr.at[hh], partner).wait_recv()

        def add(q, _):
            m, rest = q // 8, q % 8
            a, b = rest // 4, rest % 4
            fb[k, m, a, b] = (fb[k, m, a, b].astype(F32) + r1[hh, m, a, b].astype(F32)).astype(BF16)
            return 0

        lax.fori_loop(0, 16, add, 0)

        @pl.when(c == 0)
        def _():
            for i in range(1, 4):
                stage_one(hh, i, fb.at[k, :, :, (u + i) % 4]).start()

        @pl.when(c == 1)
        def _():
            for i in range(1, 4):
                stage_one(hh, i, fb.at[k, :, :, :, (u + i) % 4]).start()

    def stage_two(hh, i):
        return remote(
            s2.at[hh, :, :, (v + i) % 4], r3.at[hh, i - 1], s2s.at[hh, i], s2r.at[hh, i], b_peers[i]
        )

    def middle_sum(hh):
        k = 2 * hh + c
        for i in range(1, 4):
            stage_one(hh, i, r2.at[hh, i - 1]).wait_recv()

        def add_with(load):
            def add(q, _):
                m, rest = q // 8, q % 8
                a, b = rest // 4, rest % 4
                value = load(m, a, b).astype(F32)
                for i in range(3):
                    value = value + r2[hh, i, m, a, b].astype(F32)
                s2[hh, m, a, b] = value.astype(BF16)
                return 0

            lax.fori_loop(0, 16, add, 0)

        @pl.when(c == 0)
        def _():
            add_with(lambda m, a, b: fb[k, m, a, u, b])

        @pl.when(c == 1)
        def _():
            add_with(lambda m, a, b: fb[k, m, a, b, u])

        for i in range(1, 4):
            stage_two(hh, i).start()

    def last_sum(hh):
        for i in range(1, 4):
            stage_two(hh, i).wait_recv()
        for m in range(2):
            for a in range(2):
                value = s2[hh, m, a, v].astype(F32)
                for i in range(3):
                    value = value + r3[hh, i, m, a].astype(F32)
                s3[hh, a, m] = value.astype(BF16)

    for k in (3, 2, 1, 0):
        hk = hid[k]
        sk = scale[k][:, 0:1]
        gh = (ga * gelu_slope(hk)).astype(BF16)
        ghf = gh.astype(F32)
        mean = jnp.sum(ghf * hk, axis=1, keepdims=True) * (1.0 / D)
        gh2 = (ghf * ghf).astype(BF16)
        af = act[k].astype(F32)
        a2 = (af * af).astype(BF16)

        def step(f, acc, k=k, gh=gh, sk=sk, mean=mean):
            nf = x[k, :, cols(f)].astype(F32) * sk
            gf = g[:, cols(f)].astype(F32)
            n2[:, cols(f)] = (nf * nf).astype(BF16)
            g2[:, cols(f)] = (gf * gf).astype(BF16)
            if k == 0:
                return acc
            back = dot_nt(gh, w[k, 0, cols(f), :])
            gy = (gf + sk * (back - nf * mean)).astype(BF16)
            g[:, cols(f)] = gy
            return acc + dot_nn(gy, w[k - 1, 1, cols(f), :])

        ga = lax.fori_loop(0, D // TILE, step, zero)

        def outer(b, _, k=k, gh2=gh2, a2=a2):
            a = b // 2
            half = pl.ds((b % 2) * 2, 2)
            fd = dot_tn(n2[:, cols(b, BLK)], gh2).astype(BF16)
            fb[k, 0, a, half] = fd.reshape(2, 4, 144, 128)
            fu = dot_tn(g2[:, cols(b, BLK)], a2).astype(BF16)
            fb[k, 1, a, half] = fu.reshape(2, 4, 144, 128)
            return 0

        lax.fori_loop(0, 4, outer, 0)

        @pl.when(c != k % 2)
        def _(k=k):
            keep_or_send(k).start()

        if k == 2:

            @pl.when(c == 1)
            def _():
                open_sum(1)

        if k == 1:

            @pl.when(c == 0)
            def _():
                open_sum(1)

    open_sum(0)
    middle_sum(1)
    last_sum(1)
    middle_sum(0)
    last_sum(0)

    y_sends = []
    for i in range(1, 4):
        y_ = (y + i) % 4
        copy = remote(s3.at[y_ // 2, y_ % 2], r4.at[i], ys.at[i], yr.at[i], y_peers[i])
        copy.start()
        y_sends.append(copy)
    r4[0] = s3[h, yl]
    for copy in y_sends:
        copy.wait()
    den = jnp.zeros((2, 144, 128), F32)
    num = jnp.zeros((2, 144, 128), F32)
    for i in range(4):
        t = (y + 4 - i) % 4
        value = r4[i].astype(F32)
        den = den + value
        num = num + value * wd[t].astype(F32)
    den = den + merge_eps
    flog_out[...] = jnp.log(den)
    merged[:, yl, xx, zz] = (num / den).astype(BF16)

    neighbour = at(h, c, 1 - yl, xx, zz)
    near = remote(merged.at[:, yl, xx, zz], merged.at[:, yl, xx, zz], gs.at[0], gr.at[0], neighbour)
    near.start()
    near.wait()

    def two(u_, v_):
        return merged.at[:, :, u_ * (1 - c) + v_ * c, v_ * (1 - c) + u_ * c]

    g_sends = []
    for i in range(1, 4):
        copy = remote(two(u, v), two(u, v), gs.at[i], gr.at[i], a_peers[i])
        copy.start()
        g_sends.append(copy)
    for i in range(4):
        from_u = (u + 4 - i) % 4
        if i:
            remote(two(from_u, v), two(from_u, v), gs.at[i], gr.at[i], a_peers[i]).wait_recv()
        for j in range(1, 4):
            copy = remote(two(from_u, v), two(from_u, v), gs.at[4 * j + i], gr.at[4 * j + i], b_peers[j])
            copy.start()
            g_sends.append(copy)
    for i in range(4):
        from_u = (u + 4 - i) % 4
        for j in range(1, 4):
            from_v = (v + 4 - j) % 4
            remote(two(from_u, from_v), two(from_u, from_v), gs.at[4 * j + i], gr.at[4 * j + i], b_peers[j]).wait_recv()
    for copy in g_sends:
        copy.wait_send()

    to_next = remote(eval_out, vin, vs.at[0], vr.at[0], partner)
    to_after = remote(eval_out, vin, vs.at[0], vr.at[0], after)

    @pl.when(s == 0)
    def _():
        eval_load.wait()

    @pl.when(s != 0)
    def _():
        to_next.wait_recv()

    def weights(m, b):
        return merged[m, b // 2, pl.ds((b % 2) * 2, 2)].reshape(BLK, 128)

    small = jnp.zeros((ROWS, 128), F32)

    def eval_in(b, carry):
        total, acc = carry
        vt = vin[:, cols(b, BLK)]
        vf = vt.astype(F32)
        return total + lane_fold(vf * vf), acc + dot_nn(vt, weights(0, b))

    total, acc = lax.fori_loop(0, 4, eval_in, (small, small))
    sv = lax.rsqrt(jnp.sum(total, axis=1, keepdims=True) * (1.0 / D) + norm_eps)
    av = gelu_value(sv * acc).astype(BF16)

    def eval_step(b, _):
        eval_out[:, cols(b, BLK)] = (
            vin[:, cols(b, BLK)].astype(F32) + dot_nt(av, weights(1, b))
        ).astype(BF16)
        return 0

    lax.fori_loop(0, 4, eval_step, 0)

    @pl.when((s == 0) | (s == 2))
    def _():
        to_next.start()
        to_next.wait_send()

    @pl.when(s == 1)
    def _():
        to_after.start()
        to_after.wait_send()

    for hh in range(2):

        @pl.when(c == 1)
        def _(hh=hh):
            keep_or_send(2 * hh).wait_send()

        @pl.when(c == 0)
        def _(hh=hh):
            keep_or_send(2 * hh + 1).wait_send()

        for i in range(1, 4):
            stage_one(hh, i, r2.at[hh, i - 1]).wait_send()
            stage_two(hh, i).wait_send()

    @pl.when(c != yl)
    def _():
        give.wait()

    @pl.when(c == yl)
    def _():
        hold.wait()


def local(entry_states, down_proj, up_proj, label_rows, sampled_labels, eval_states):
    vmem = pl.BlockSpec(memory_space=pltpu.VMEM)
    hbm = pl.BlockSpec(memory_space=pl.ANY)
    dma = pltpu.SemaphoreType.DMA
    labels = jnp.broadcast_to(sampled_labels.reshape(TASKS, N, 1), (TASKS, N, 128))
    eval_out, logp, flog = pl.pallas_call(
        kernel,
        out_shape=(
            jax.ShapeDtypeStruct((ROWS, D), BF16),
            jax.ShapeDtypeStruct((N, 128), F32),
            jax.ShapeDtypeStruct((2, 144, 128), F32),
        ),
        in_specs=[hbm] * 6,
        out_specs=(vmem, vmem, vmem),
        scratch_shapes=[
            pltpu.VMEM((4, 2, D, R), BF16),
            pltpu.VMEM((5, N, D), BF16),
            pltpu.VMEM((N, D), BF16),
            pltpu.VMEM((LABELS, D), BF16),
            pltpu.VMEM((N, 128), jnp.int32),
            pltpu.VMEM((N, D), BF16),
            pltpu.VMEM((N, D), BF16),
            pltpu.VMEM((4, N, R), F32),
            pltpu.VMEM((4, N, R), BF16),
            pltpu.VMEM((4, N, 128), F32),
            pltpu.VMEM((4, 2, 2, 4, 4, 144, 128), BF16),
            pltpu.VMEM((2, 2, 2, 4, 4, 144, 128), BF16),
            pltpu.VMEM((2, 3, 2, 2, 4, 144, 128), BF16),
            pltpu.VMEM((2, 2, 2, 4, 144, 128), BF16),
            pltpu.VMEM((2, 3, 2, 2, 144, 128), BF16),
            pltpu.VMEM((2, 2, 2, 144, 128), BF16),
            pltpu.VMEM((4, 2, 144, 128), BF16),
            pltpu.VMEM((4, 2, 144, 128), BF16),
            pltpu.VMEM((2, 2, 4, 4, 144, 128), BF16),
            pltpu.VMEM((ROWS, D), BF16),
            pltpu.VMEM((N, 128), F32),
            dma((16,)),
            dma((2,)), dma((2,)),
            dma((2,)), dma((2,)),
            dma((4,)), dma((4,)),
            dma((4, 4)), dma((4, 4)),
            dma((4,)), dma((4,)),
            dma((3,)), dma((3,)),
            dma((2,)), dma((2,)),
            dma((2, 4)), dma((2, 4)),
            dma((2, 4)), dma((2, 4)),
            dma((4,)), dma((4,)),
            dma((16,)), dma((16,)),
            dma((1,)), dma((1,)),
        ],
        compiler_params=pltpu.CompilerParams(
            collective_id=0, has_side_effects=True, vmem_limit_bytes=67043328
        ),
        name="merge",
    )(
        down_proj.reshape(TASKS, D, R),
        up_proj.reshape(TASKS, D, R),
        entry_states.reshape(N, D),
        labels,
        label_rows,
        eval_states,
    )
    return (
        eval_out[None],
        logp[:, 0].reshape(1, MICRO, ROWS),
        flog[None],
    )


def solution(mesh):
    placed = (
        P(None, "dp", None),
        P("section", None, None, None),
        P("section", None, None, None),
        P(),
        P(None, None, "dp"),
        P("dp", None),
    )
    return jax.shard_map(
        local,
        mesh=mesh,
        in_specs=placed,
        out_specs=(
            P("section", "dp", None),
            P("section", None, "dp"),
            P("section", None, "dp", None),
        ),
        check_vma=False,
    )
```

time: 896 us -> 164 us (0.18)
  waiting for transfers between devices: 343 us -> 0 us
  matrix products: 220 us -> 0 us
  other arithmetic: 184 us -> 0 us
  Pallas kernels: 0 us -> 155 us
  local copies, waits for them, and re-layouts: 74.8 us -> 6.58 us
  starting transfers between devices: 51.3 us -> 0 us
  between operations: 14.2 us -> 0.65 us
    dot_general x61 -> x0, matrix products: 220 us -> none  [the longest x20 86.2 us: block_forward(): jnp.einsum('tnr,tdr->tnd', active, w_up, preferred_element_type=jnp.float32)]
    reduce_scatter x1 -> x0, waiting for transfers between devices: 171 us -> none  [in_one_piece(): lax.psum_scatter(both, axis, scatter_dimension=dim, tiled=True)]
    pallas_call x0 -> x1, Pallas kernels: none -> 155 us  [local(): pl.pallas_call(kernel, out_shape=(jax.ShapeDtypeStruct((ROWS, D), BF16),...]
    ppermute x19 -> x0, waiting for transfers between devices: 149 us -> none  [from_behind(): return lax.ppermute(block, axis, route)]
    dynamic_update_slice x32 -> x0, other arithmetic: 60.6 us -> none  [the longest x8 29.6 us: backward_turn(): lax.dynamic_update_index_in_dim(wide_all, jnp.where(active_turn, wide_squ...]
    reduce_sum x38 -> x0, other arithmetic: 41.8 us -> none  [the longest x20 18.1 us: block_forward(): jnp.mean(state_float * state_float, axis=-1, keepdims=True) + norm_eps]
    convert_element_type x16 -> x0, other arithmetic: 36 us -> none  [the longest x8 23.7 us: block_backward(): grad_in = (grad_float + norm_scale * (grad_norm - norm_float * jnp.mean(g...]
    ppermute x19 -> x0, starting transfers between devices: 35.4 us -> none  [from_behind(): return lax.ppermute(block, axis, route)]
  transfers between devices with their start and end apart: 22 -> 0, of which waited for: 13 -> 0; matrix products, arithmetic and copies ran while one was open for 11% -> 0% of each run, Pallas kernels for 0% -> 0%
where the time goes in v1:
time: 164 us; the launch traced here: 162 us
  Pallas kernels  155 us (95%)
  local copies, waits for them, and re-layouts  6.58 us (4%)
    pallas_call x1, Pallas kernels, local(): pl.pallas_call(kernel, out_shape=(jax.ShapeDtypeStruct((ROWS, D), BF16),...  155 us
    unnamed x3, local copies, waits for them, and re-layouts  3.98 us

profile of v1, /device:TPU:17, one launch (start us, length us, event | category | flops | bytes accessed | tf_op | source)
XLA Modules:
  0.0 162.1 jit_solution(1282046664015976691)
XLA Ops:
  0.6 0.7 copy.10
  1.3 0.1 broadcast_in_dim.13
  1.4 0.9 broadcast_in_dim.14.labels
  2.3 154.9 %merge.1 = (bf16[32,4608]{1,0:T(8,128)(2,1)}, f32[160,128]{1,0:T(8,128)}, f32[2,144,128]{2,1,0:T(8,128)}) custom-call(bf16[4,4608,128]{2,1,0:T(8,128)(2,1)} %bitcast.5, bf16[4,4608,128]{2,1,0:T(8,128)(2,1)} %bitcast.6, bf16[160,4608]{1,0:T(8,128)(2,1)} %bitcast.7, s32[4,160,128]{2,1,0:T(8,128)} %broadcast_in_dim.14.labels, bf16[256,4608]{1,0:T(8,128)(2,1)} %label_rows.1, ...), custom_call_target="tpu_custom_call" | custom-call | tf_op jit(solution)/shard_map/merge/pallas_call | solution.py:528
  157.2 1.0 slice_reduce_fusion
  158.2 0.7 reshape_squeeze.4
  158.9 1.7 %copy.14 = bf16[1,32,4608]{2,1,0:T(8,128)(2,1)} copy(bf16[1,32,4608]{2,1,0:T(8,128)(2,1)} %bitcast.8) | data formatting | bytes 589824
  160.6 1.6 copy.15

commit v2 on v1

--- a/solution.py
+++ b/solution.py
@@ -49,6 +49,12 @@
     return lax.dot_general(a, b, (((0,), (0,)), ((), ())), preferred_element_type=F32)
 
 
+def over(count, body, carry):
+    for i in range(count):
+        carry = body(i, carry)
+    return carry
+
+
 def lane_fold(v):
     total = v[:, 0:128]
     for i in range(1, v.shape[1] // 128):
@@ -59,7 +65,7 @@
 def kernel(
     down, up, entry, labels, label_rows, evals,
     eval_out, logp_out, flog_out,
-    w, x, g, rows, lab, n2, g2, hid, act, scale,
+    w, x, g, rows, lab, wide, narrow, hid, act, scale,
     fb, r1, r2, s2, r3, s3, r4, wd, merged, vin, picked,
     load_sem, ps, pr, cs, cr, as_, ar, bs, br, os_, orr, es, er, fs, fr,
     s1s, s1r, s2s, s2r, ys, yr, gs, gr, vs, vr,
@@ -81,13 +87,14 @@
     def at_uv(u_, v_):
         return at(h, c, yl, u_ * (1 - c) + v_ * c, v_ * (1 - c) + u_ * c)
 
-    def at_y(y_):
-        return at(y_ // 2, c, y_ % 2, xx, zz)
+    def at_y(y_, core=None):
+        return at(y_ // 2, c if core is None else core, y_ % 2, xx, zz)
 
     partner = at(h, 1 - c, yl, xx, zz)
     swap = at(h, 1 - c, 1 - yl, xx, zz)
     across = at(1 - h, c, 1 - yl, xx, zz)
     after = at(1 - h, 1 - c, yl, xx, zz)
+    third = at(1 - h, 1 - c, 1 - yl, xx, zz)
     a_peers = [None] + [at_uv((u + i) % 4, v) for i in range(1, 4)]
     b_peers = [None] + [at_uv(u, (v + i) % 4) for i in range(1, 4)]
     y_peers = [None] + [at_y((y + i) % 4) for i in range(1, 4)]
@@ -98,7 +105,7 @@
         )
 
     barrier = pltpu.get_barrier_semaphore()
-    everyone = [partner, swap, after] + a_peers[1:] + b_peers[1:] + y_peers[1:]
+    everyone = [partner, swap, after, third] + a_peers[1:] + b_peers[1:] + y_peers[1:]
     for peer in everyone:
         pl.semaphore_signal(barrier, inc=1, device_id=peer, device_id_type=MESH)
     pl.semaphore_wait(barrier, len(everyone))
@@ -211,7 +218,7 @@
     zero = jnp.zeros((N, 128), F32)
 
     def cols(f, size=TILE):
-        return pl.ds(pl.multiple_of(f * size, size), size)
+        return pl.ds(f * size, size)
 
     def first(f, carry):
         total, acc = carry
@@ -219,7 +226,7 @@
         xf = xt.astype(F32)
         return total + lane_fold(xf * xf), acc + dot_nn(xt, w[0, 0, cols(f), :])
 
-    total, acc = lax.fori_loop(0, D // TILE, first, (zero, zero))
+    total, acc = over(D // TILE, first, (zero, zero))
     for k in range(4):
         sk = lax.rsqrt(jnp.sum(total, axis=1, keepdims=True) * (1.0 / D) + norm_eps)
         hk = sk * acc
@@ -240,7 +247,7 @@
             return total + lane_fold(nf * nf), acc + more
 
         width = R if k < 3 else LABELS
-        total, acc = lax.fori_loop(0, D // TILE, step, (zero, jnp.zeros((N, width), F32)))
+        total, acc = over(D // TILE, step, (zero, jnp.zeros((N, width), F32)))
 
     sy = lax.rsqrt(jnp.sum(total, axis=1, keepdims=True) * (1.0 / D) + norm_eps)
     logits = sy * acc
@@ -271,81 +278,64 @@
         g[:, cols(f)] = gy
         return acc + dot_nn(gy, w[3, 1, cols(f), :])
 
-    ga = lax.fori_loop(0, D // TILE, head, zero)
-
-    def keep_or_send(k):
-        return remote(fb.at[k], r1.at[k // 2], fs.at[k // 2], fr.at[k // 2], partner)
-
-    def source(hh, q):
-        return fb.at[2 * hh + c, :, :, q], fb.at[2 * hh + c, :, :, :, q]
-
-    def stage_one(hh, i, view):
-        return remote(view, r2.at[hh, i - 1], s1s.at[hh, i], s1r.at[hh, i], a_peers[i])
-
-    def open_sum(hh):
-        k = 2 * hh + c
-        remote(fb.at[k], r1.at[hh], fs.at[hh], fr.at[hh], partner).wait_recv()
-
-        def add(q, _):
-            m, rest = q // 8, q % 8
-            a, b = rest // 4, rest % 4
-            fb[k, m, a, b] = (fb[k, m, a, b].astype(F32) + r1[hh, m, a, b].astype(F32)).astype(BF16)
-            return 0
-
-        lax.fori_loop(0, 16, add, 0)
+    ga = over(D // TILE, head, zero)
+
+    def give_half(k):
+        return remote(fb.at[k, 1 - c], r1.at[k], fs.at[k], fr.at[k], partner)
+
+    def stage_one(k, i, view):
+        return remote(view, r2.at[k, i - 1], s1s.at[k, i], s1r.at[k, i], a_peers[i])
+
+    def open_sum(k):
+        remote(fb.at[k, c], r1.at[k], fs.at[k], fr.at[k], partner).wait_recv()
+        for a in range(2):
+            for b in range(4):
+                fb[k, c, a, b] = (fb[k, c, a, b].astype(F32) + r1[k, a, b].astype(F32)).astype(BF16)
 
         @pl.when(c == 0)
         def _():
-            for i in range(1, 4):
-                stage_one(hh, i, fb.at[k, :, :, (u + i) % 4]).start()
+            for i in (2, 1, 3):
+                stage_one(k, i, fb.at[k, 0, :, (u + i) % 4]).start()
 
         @pl.when(c == 1)
         def _():
-            for i in range(1, 4):
-                stage_one(hh, i, fb.at[k, :, :, :, (u + i) % 4]).start()
-
-    def stage_two(hh, i):
-        return remote(
-            s2.at[hh, :, :, (v + i) % 4], r3.at[hh, i - 1], s2s.at[hh, i], s2r.at[hh, i], b_peers[i]
-        )
-
-    def middle_sum(hh):
-        k = 2 * hh + c
+            for i in (2, 1, 3):
+                stage_one(k, i, fb.at[k, 1, :, :, (u + i) % 4]).start()
+
+    def stage_two(k, i):
+        return remote(s2.at[k, :, (v + i) % 4], r3.at[k, i - 1], s2s.at[k, i], s2r.at[k, i], b_peers[i])
+
+    def middle_sum(k):
         for i in range(1, 4):
-            stage_one(hh, i, r2.at[hh, i - 1]).wait_recv()
+            stage_one(k, i, r2.at[k, i - 1]).wait_recv()
 
         def add_with(load):
-            def add(q, _):
-                m, rest = q // 8, q % 8
-                a, b = rest // 4, rest % 4
-                value = load(m, a, b).astype(F32)
-                for i in range(3):
-                    value = value + r2[hh, i, m, a, b].astype(F32)
-                s2[hh, m, a, b] = value.astype(BF16)
-                return 0
-
-            lax.fori_loop(0, 16, add, 0)
+            for a in range(2):
+                for b in range(4):
+                    value = load(a, b).astype(F32)
+                    for i in range(3):
+                        value = value + r2[k, i, a, b].astype(F32)
+                    s2[k, a, b] = value.astype(BF16)
 
         @pl.when(c == 0)
         def _():
-            add_with(lambda m, a, b: fb[k, m, a, u, b])
+            add_with(lambda a, b: fb[k, 0, a, u, b])
 
         @pl.when(c == 1)
         def _():
-            add_with(lambda m, a, b: fb[k, m, a, b, u])
-
+            add_with(lambda a, b: fb[k, 1, a, b, u])
+
+        for i in (2, 1, 3):
+            stage_two(k, i).start()
+
+    def last_sum(k):
         for i in range(1, 4):
-            stage_two(hh, i).start()
-
-    def last_sum(hh):
-        for i in range(1, 4):
-            stage_two(hh, i).wait_recv()
-        for m in range(2):
-            for a in range(2):
-                value = s2[hh, m, a, v].astype(F32)
-                for i in range(3):
-                    value = value + r3[hh, i, m, a].astype(F32)
-                s3[hh, a, m] = value.astype(BF16)
+            stage_two(k, i).wait_recv()
+        for a in range(2):
+            value = s2[k, a, v].astype(F32)
+            for i in range(3):
+                value = value + r3[k, i, a].astype(F32)
+            s3[k, a] = value.astype(BF16)
 
     for k in (3, 2, 1, 0):
         hk = hid[k]
@@ -353,15 +343,15 @@
         gh = (ga * gelu_slope(hk)).astype(BF16)
         ghf = gh.astype(F32)
         mean = jnp.sum(ghf * hk, axis=1, keepdims=True) * (1.0 / D)
-        gh2 = (ghf * ghf).astype(BF16)
+        narrow[0] = (ghf * ghf).astype(BF16)
         af = act[k].astype(F32)
-        a2 = (af * af).astype(BF16)
+        narrow[1] = (af * af).astype(BF16)
 
         def step(f, acc, k=k, gh=gh, sk=sk, mean=mean):
             nf = x[k, :, cols(f)].astype(F32) * sk
             gf = g[:, cols(f)].astype(F32)
-            n2[:, cols(f)] = (nf * nf).astype(BF16)
-            g2[:, cols(f)] = (gf * gf).astype(BF16)
+            wide[0, :, cols(f)] = (nf * nf).astype(BF16)
+            wide[1, :, cols(f)] = (gf * gf).astype(BF16)
             if k == 0:
                 return acc
             back = dot_nt(gh, w[k, 0, cols(f), :])
@@ -369,48 +359,40 @@
             g[:, cols(f)] = gy
             return acc + dot_nn(gy, w[k - 1, 1, cols(f), :])
 
-        ga = lax.fori_loop(0, D // TILE, step, zero)
-
-        def outer(b, _, k=k, gh2=gh2, a2=a2):
-            a = b // 2
-            half = pl.ds((b % 2) * 2, 2)
-            fd = dot_tn(n2[:, cols(b, BLK)], gh2).astype(BF16)
-            fb[k, 0, a, half] = fd.reshape(2, 4, 144, 128)
-            fu = dot_tn(g2[:, cols(b, BLK)], a2).astype(BF16)
-            fb[k, 1, a, half] = fu.reshape(2, 4, 144, 128)
-            return 0
-
-        lax.fori_loop(0, 4, outer, 0)
-
-        @pl.when(c != k % 2)
-        def _(k=k):
-            keep_or_send(k).start()
-
-        if k == 2:
-
-            @pl.when(c == 1)
-            def _():
-                open_sum(1)
-
-        if k == 1:
-
-            @pl.when(c == 0)
-            def _():
-                open_sum(1)
+        ga = over(D // TILE, step, zero)
+        if k < 3:
+            open_sum(k + 1)
+        for m in (1 - c, c):
+            thin = narrow[m]
+            for b in range(4):
+                value = dot_tn(wide[m, :, cols(b, BLK)], thin).astype(BF16)
+                fb[k, m, b // 2, pl.ds((b % 2) * 2, 2)] = value.reshape(2, 4, 144, 128)
+            if m is not c:
+                give_half(k).start()
+        if k < 2:
+            middle_sum(k + 2)
 
     open_sum(0)
+    last_sum(3)
     middle_sum(1)
+    last_sum(2)
+    middle_sum(0)
     last_sum(1)
-    middle_sum(0)
     last_sum(0)
 
     y_sends = []
-    for i in range(1, 4):
+    for i in range(4):
         y_ = (y + i) % 4
-        copy = remote(s3.at[y_ // 2, y_ % 2], r4.at[i], ys.at[i], yr.at[i], y_peers[i])
-        copy.start()
-        y_sends.append(copy)
-    r4[0] = s3[h, yl]
+        for j in range(2):
+            core = (c + j) % 2
+            if i or j:
+                copy = remote(
+                    s3.at[2 * (y_ // 2) + core, y_ % 2], r4.at[i, c],
+                    ys.at[i, j], yr.at[i, j], at_y(y_, core),
+                )
+                copy.start()
+                y_sends.append(copy)
+    r4[0, c] = s3[s, yl]
     for copy in y_sends:
         copy.wait()
     den = jnp.zeros((2, 144, 128), F32)
@@ -453,63 +435,54 @@
     for copy in g_sends:
         copy.wait_send()
 
-    to_next = remote(eval_out, vin, vs.at[0], vr.at[0], partner)
-    to_after = remote(eval_out, vin, vs.at[0], vr.at[0], after)
+    def hand_on(b, to):
+        return remote(eval_out.at[:, cols(b, BLK)], vin.at[:, cols(b, BLK)], vs.at[b], vr.at[b], to)
 
     @pl.when(s == 0)
     def _():
         eval_load.wait()
-
-    @pl.when(s != 0)
-    def _():
-        to_next.wait_recv()
 
     def weights(m, b):
         return merged[m, b // 2, pl.ds((b % 2) * 2, 2)].reshape(BLK, 128)
 
-    small = jnp.zeros((ROWS, 128), F32)
-
-    def eval_in(b, carry):
-        total, acc = carry
+    total = jnp.zeros((ROWS, 128), F32)
+    acc = jnp.zeros((ROWS, 128), F32)
+    for b in range(4):
+
+        @pl.when(s != 0)
+        def _(b=b):
+            hand_on(b, partner).wait_recv()
+
         vt = vin[:, cols(b, BLK)]
         vf = vt.astype(F32)
-        return total + lane_fold(vf * vf), acc + dot_nn(vt, weights(0, b))
-
-    total, acc = lax.fori_loop(0, 4, eval_in, (small, small))
+        total = total + lane_fold(vf * vf)
+        acc = acc + dot_nn(vt, weights(0, b))
     sv = lax.rsqrt(jnp.sum(total, axis=1, keepdims=True) * (1.0 / D) + norm_eps)
     av = gelu_value(sv * acc).astype(BF16)
-
-    def eval_step(b, _):
+    for b in range(4):
         eval_out[:, cols(b, BLK)] = (
             vin[:, cols(b, BLK)].astype(F32) + dot_nt(av, weights(1, b))
         ).astype(BF16)
-        return 0
-
-    lax.fori_loop(0, 4, eval_step, 0)
-
-    @pl.when((s == 0) | (s == 2))
-    def _():
-        to_next.start()
-        to_next.wait_send()
-
-    @pl.when(s == 1)
-    def _():
-        to_after.start()
-        to_after.wait_send()
-
-    for hh in range(2):
-
-        @pl.when(c == 1)
-        def _(hh=hh):
-            keep_or_send(2 * hh).wait_send()
 
         @pl.when(c == 0)
-        def _(hh=hh):
-            keep_or_send(2 * hh + 1).wait_send()
-
+        def _(b=b):
+            hand_on(b, partner).start()
+
+        @pl.when(s == 1)
+        def _(b=b):
+            hand_on(b, after).start()
+
+    for b in range(4):
+
+        @pl.when(s != 3)
+        def _(b=b):
+            hand_on(b, partner).wait_send()
+
+    for k in range(4):
+        give_half(k).wait_send()
         for i in range(1, 4):
-            stage_one(hh, i, r2.at[hh, i - 1]).wait_send()
-            stage_two(hh, i).wait_send()
+            stage_one(k, i, r2.at[k, i - 1]).wait_send()
+            stage_two(k, i).wait_send()
 
     @pl.when(c != yl)
     def _():
@@ -540,17 +513,17 @@
             pltpu.VMEM((N, D), BF16),
             pltpu.VMEM((LABELS, D), BF16),
             pltpu.VMEM((N, 128), jnp.int32),
-            pltpu.VMEM((N, D), BF16),
-            pltpu.VMEM((N, D), BF16),
+            pltpu.VMEM((2, N, D), BF16),
+            pltpu.VMEM((2, N, R), BF16),
             pltpu.VMEM((4, N, R), F32),
             pltpu.VMEM((4, N, R), BF16),
             pltpu.VMEM((4, N, 128), F32),
             pltpu.VMEM((4, 2, 2, 4, 4, 144, 128), BF16),
-            pltpu.VMEM((2, 2, 2, 4, 4, 144, 128), BF16),
-            pltpu.VMEM((2, 3, 2, 2, 4, 144, 128), BF16),
-            pltpu.VMEM((2, 2, 2, 4, 144, 128), BF16),
-            pltpu.VMEM((2, 3, 2, 2, 144, 128), BF16),
-            pltpu.VMEM((2, 2, 2, 144, 128), BF16),
+            pltpu.VMEM((4, 2, 4, 4, 144, 128), BF16),
+            pltpu.VMEM((4, 3, 2, 4, 144, 128), BF16),
+            pltpu.VMEM((4, 2, 4, 144, 128), BF16),
+            pltpu.VMEM((4, 3, 2, 144, 128), BF16),
+            pltpu.VMEM((4, 2, 144, 128), BF16),
             pltpu.VMEM((4, 2, 144, 128), BF16),
             pltpu.VMEM((4, 2, 144, 128), BF16),
             pltpu.VMEM((2, 2, 4, 4, 144, 128), BF16),
@@ -563,12 +536,12 @@
             dma((4, 4)), dma((4, 4)),
             dma((4,)), dma((4,)),
             dma((3,)), dma((3,)),
-            dma((2,)), dma((2,)),
-            dma((2, 4)), dma((2, 4)),
-            dma((2, 4)), dma((2, 4)),
             dma((4,)), dma((4,)),
+            dma((4, 4)), dma((4, 4)),
+            dma((4, 4)), dma((4, 4)),
+            dma((4, 2)), dma((4, 2)),
             dma((16,)), dma((16,)),
-            dma((1,)), dma((1,)),
+            dma((4,)), dma((4,)),
         ],
         compiler_params=pltpu.CompilerParams(
             collective_id=0, has_side_effects=True, vmem_limit_bytes=67043328

time: 164 us -> 139 us (0.85)
  Pallas kernels: 155 us -> 130 us
    pallas_call x1, Pallas kernels: 155 us -> 130 us  [local(): pl.pallas_call(kernel, out_shape=(jax.ShapeDtypeStruct((ROWS, D), BF16),...]
where the time goes in v2:
time: 139 us; the launch traced here: 138 us
  Pallas kernels  130 us (94%)
  local copies, waits for them, and re-layouts  6.58 us (5%)
    pallas_call x1, Pallas kernels, local(): pl.pallas_call(kernel, out_shape=(jax.ShapeDtypeStruct((ROWS, D), BF16),...  130 us
    unnamed x3, local copies, waits for them, and re-layouts  3.98 us

profile of v2, /device:TPU:17, one launch (start us, length us, event | category | flops | bytes accessed | tf_op | source)
XLA Modules:
  0.0 137.7 jit_solution(11534001852688167942)
XLA Ops:
  0.6 0.7 copy.10
  1.3 0.1 broadcast_in_dim.13
  1.4 0.9 broadcast_in_dim.14.labels
  2.3 130.5 %merge.1 = (bf16[32,4608]{1,0:T(8,128)(2,1)}, f32[160,128]{1,0:T(8,128)}, f32[2,144,128]{2,1,0:T(8,128)}) custom-call(bf16[4,4608,128]{2,1,0:T(8,128)(2,1)} %bitcast.5, bf16[4,4608,128]{2,1,0:T(8,128)(2,1)} %bitcast.6, bf16[160,4608]{1,0:T(8,128)(2,1)} %bitcast.7, s32[4,160,128]{2,1,0:T(8,128)} %broadcast_in_dim.14.labels, bf16[256,4608]{1,0:T(8,128)(2,1)} %label_rows.1, ...), custom_call_target="tpu_custom_call" | custom-call | tf_op jit(solution)/shard_map/merge/pallas_call | solution.py:501
  132.8 1.0 slice_reduce_fusion
  133.8 0.7 reshape_squeeze.4
  134.4 1.7 %copy.14 = bf16[1,32,4608]{2,1,0:T(8,128)(2,1)} copy(bf16[1,32,4608]{2,1,0:T(8,128)(2,1)} %bitcast.8) | data formatting | bytes 589824
  136.1 1.6 %copy.15 = f32[1,2,144,128]{3,2,1,0:T(8,128)} copy(f32[1,2,144,128]{3,2,1,0:T(8,128)} %bitcast.9) | data formatting | bytes 294912

commit v3 on v2

--- a/solution.py
+++ b/solution.py
@@ -66,9 +66,9 @@
     down, up, entry, labels, label_rows, evals,
     eval_out, logp_out, flog_out,
     w, x, g, rows, lab, wide, narrow, hid, act, scale,
-    fb, r1, r2, s2, r3, s3, r4, wd, merged, vin, picked,
+    fb, r1, r2, s2, r3, s3, r4, dens, wd, merged, vin, picked,
     load_sem, ps, pr, cs, cr, as_, ar, bs, br, os_, orr, es, er, fs, fr,
-    s1s, s1r, s2s, s2r, ys, yr, gs, gr, vs, vr,
+    s1s, s1r, s2s, s2r, ys, yr, gas, gar, gbs, gbr, vs, vr,
 ):
     s = lax.axis_index("section")
     d = lax.axis_index("dp")
@@ -97,6 +97,8 @@
     third = at(1 - h, 1 - c, 1 - yl, xx, zz)
     a_peers = [None] + [at_uv((u + i) % 4, v) for i in range(1, 4)]
     b_peers = [None] + [at_uv(u, (v + i) % 4) for i in range(1, 4)]
+    x_peers = [None] + [at(h, c, yl, (xx + i) % 4, zz) for i in range(1, 4)]
+    z_peers = [None] + [at(h, c, yl, xx, (zz + i) % 4) for i in range(1, 4)]
     y_peers = [None] + [at_y((y + i) % 4) for i in range(1, 4)]
 
     def remote(src, dst, send, recv, to):
@@ -150,10 +152,12 @@
         pltpu.make_async_copy(up.at[y], w.at[s, 1], load_sem.at[3]),
         pltpu.make_async_copy(label_rows, rows, load_sem.at[4]),
     ]
-    mine = pl.ds(pl.multiple_of(d * 144, 16), 144)
     for t in range(TASKS):
-        loads.append(pltpu.make_async_copy(down.at[t, mine], wd.at[t, 0], load_sem.at[5 + 2 * t]))
-        loads.append(pltpu.make_async_copy(up.at[t, mine], wd.at[t, 1], load_sem.at[6 + 2 * t]))
+        for a in range(2):
+            mine = pl.ds(pl.multiple_of((a * 16 + xx * 4 + zz) * 144, 16), 144)
+            for m, whole in enumerate((down, up)):
+                sem = load_sem.at[16 + 4 * t + 2 * a + m]
+                loads.append(pltpu.make_async_copy(whole.at[t, mine], wd.at[t, m, a], sem))
     for copy in loads:
         copy.start()
     eval_load = pltpu.make_async_copy(evals, vin, load_sem.at[13])
@@ -272,10 +276,17 @@
     mean = jnp.sum(e.astype(F32) * logits, axis=1, keepdims=True) * (1.0 / D)
     sm = sy * mean
 
+    def squares(k, f, gy):
+        nf = x[k, :, cols(f)].astype(F32) * scale[k][:, 0:1]
+        gf = gy.astype(F32)
+        wide[0, :, cols(f)] = (nf * nf).astype(BF16)
+        wide[1, :, cols(f)] = (gf * gf).astype(BF16)
+
     def head(f, acc):
         back = dot_nn(e, rows[:, cols(f)])
         gy = (sy * (back - x[4, :, cols(f)].astype(F32) * sm)).astype(BF16)
         g[:, cols(f)] = gy
+        squares(3, f, gy)
         return acc + dot_nn(gy, w[3, 1, cols(f), :])
 
     ga = over(D // TILE, head, zero)
@@ -327,6 +338,14 @@
 
         for i in (2, 1, 3):
             stage_two(k, i).start()
+
+    def along_y(k, q):
+        y_ = 2 * (k // 2) + q
+        slot = (y_ + 4 - y) % 4
+        return remote(s3.at[k], r4.at[slot, c], ys.at[k, q], yr.at[slot, c], at(k // 2, k % 2, q, xx, zz))
+
+    def is_me(k, q):
+        return (h == k // 2) & (c == k % 2) & (yl == q)
 
     def last_sum(k):
         for i in range(1, 4):
@@ -336,6 +355,63 @@
             for i in range(3):
                 value = value + r3[k, i, a].astype(F32)
             s3[k, a] = value.astype(BF16)
+        for q in range(2):
+
+            @pl.when(jnp.logical_not(is_me(k, q)))
+            def _(q=q):
+                along_y(k, q).start()
+
+            @pl.when(is_me(k, q))
+            def _():
+                r4[0, c] = s3[k]
+
+    def block(m, x_, z_):
+        return merged.at[m, :, x_, z_]
+
+    def gather_a(m, i):
+        peers = (x_peers, z_peers)[m]
+        return remote(block(m, xx, zz), block(m, xx, zz), gas.at[m, i], gar.at[m, i], peers[i])
+
+    def gather_b(m, i, j):
+        x_ = (xx + 4 - i) % 4 if m == 0 else xx
+        z_ = (zz + 4 - i) % 4 if m == 1 else zz
+        peers = (z_peers, x_peers)[m]
+        return remote(block(m, x_, z_), block(m, x_, z_), gbs.at[m, i, j], gbr.at[m, i, j], peers[j])
+
+    def merge():
+        for i in range(4):
+            for m in range(2):
+                arrived = remote(r4.at[i, m], r4.at[i, m], ys.at[0, 0], yr.at[i, m], partner)
+                if i:
+                    arrived.wait_recv()
+                else:
+
+                    @pl.when(c != m)
+                    def _(arrived=arrived):
+                        arrived.wait_recv()
+
+        for m in range(2):
+            for a in range(2):
+                den = jnp.zeros((144, 128), F32)
+                num = jnp.zeros((144, 128), F32)
+                for i in range(4):
+                    t = (y + 4 - i) % 4
+                    value = r4[i, m, a].astype(F32)
+                    den = den + value
+                    num = num + value * wd[t, m, a].astype(F32)
+                den = den + merge_eps
+                dens[a, m] = den
+                merged[m, a, xx, zz] = (num / den).astype(BF16)
+            for i in (1, 3, 2):
+                gather_a(m, i).start()
+
+    def pass_on():
+        for i in (0, 1, 3, 2):
+            for m in range(2):
+                if i:
+                    gather_a(m, i).wait_recv()
+                for j in (1, 3, 2):
+                    gather_b(m, i, j).start()
 
     for k in (3, 2, 1, 0):
         hk = hid[k]
@@ -347,21 +423,6 @@
         af = act[k].astype(F32)
         narrow[1] = (af * af).astype(BF16)
 
-        def step(f, acc, k=k, gh=gh, sk=sk, mean=mean):
-            nf = x[k, :, cols(f)].astype(F32) * sk
-            gf = g[:, cols(f)].astype(F32)
-            wide[0, :, cols(f)] = (nf * nf).astype(BF16)
-            wide[1, :, cols(f)] = (gf * gf).astype(BF16)
-            if k == 0:
-                return acc
-            back = dot_nt(gh, w[k, 0, cols(f), :])
-            gy = (gf + sk * (back - nf * mean)).astype(BF16)
-            g[:, cols(f)] = gy
-            return acc + dot_nn(gy, w[k - 1, 1, cols(f), :])
-
-        ga = over(D // TILE, step, zero)
-        if k < 3:
-            open_sum(k + 1)
         for m in (1 - c, c):
             thin = narrow[m]
             for b in range(4):
@@ -369,71 +430,41 @@
                 fb[k, m, b // 2, pl.ds((b % 2) * 2, 2)] = value.reshape(2, 4, 144, 128)
             if m is not c:
                 give_half(k).start()
-        if k < 2:
-            middle_sum(k + 2)
-
+        if k == 0:
+            break
+
+        def step(f, acc, k=k, gh=gh, sk=sk, sm=sk * mean):
+            back = dot_nt(gh, w[k, 0, cols(f), :])
+            gy = (
+                g[:, cols(f)].astype(F32) + (sk * back - x[k, :, cols(f)].astype(F32) * (sk * sm))
+            ).astype(BF16)
+            g[:, cols(f)] = gy
+            squares(k - 1, f, gy)
+            return acc + dot_nn(gy, w[k - 1, 1, cols(f), :])
+
+        ga = over(D // TILE, step, zero)
+        open_sum(k)
+
+    middle_sum(3)
     open_sum(0)
     last_sum(3)
+    middle_sum(2)
+    last_sum(2)
     middle_sum(1)
-    last_sum(2)
+    last_sum(1)
     middle_sum(0)
-    last_sum(1)
+
+    @pl.when(s != 0)
+    def _():
+        merge()
+
     last_sum(0)
 
-    y_sends = []
-    for i in range(4):
-        y_ = (y + i) % 4
-        for j in range(2):
-            core = (c + j) % 2
-            if i or j:
-                copy = remote(
-                    s3.at[2 * (y_ // 2) + core, y_ % 2], r4.at[i, c],
-                    ys.at[i, j], yr.at[i, j], at_y(y_, core),
-                )
-                copy.start()
-                y_sends.append(copy)
-    r4[0, c] = s3[s, yl]
-    for copy in y_sends:
-        copy.wait()
-    den = jnp.zeros((2, 144, 128), F32)
-    num = jnp.zeros((2, 144, 128), F32)
-    for i in range(4):
-        t = (y + 4 - i) % 4
-        value = r4[i].astype(F32)
-        den = den + value
-        num = num + value * wd[t].astype(F32)
-    den = den + merge_eps
-    flog_out[...] = jnp.log(den)
-    merged[:, yl, xx, zz] = (num / den).astype(BF16)
-
-    neighbour = at(h, c, 1 - yl, xx, zz)
-    near = remote(merged.at[:, yl, xx, zz], merged.at[:, yl, xx, zz], gs.at[0], gr.at[0], neighbour)
-    near.start()
-    near.wait()
-
-    def two(u_, v_):
-        return merged.at[:, :, u_ * (1 - c) + v_ * c, v_ * (1 - c) + u_ * c]
-
-    g_sends = []
-    for i in range(1, 4):
-        copy = remote(two(u, v), two(u, v), gs.at[i], gr.at[i], a_peers[i])
-        copy.start()
-        g_sends.append(copy)
-    for i in range(4):
-        from_u = (u + 4 - i) % 4
-        if i:
-            remote(two(from_u, v), two(from_u, v), gs.at[i], gr.at[i], a_peers[i]).wait_recv()
-        for j in range(1, 4):
-            copy = remote(two(from_u, v), two(from_u, v), gs.at[4 * j + i], gr.at[4 * j + i], b_peers[j])
-            copy.start()
-            g_sends.append(copy)
-    for i in range(4):
-        from_u = (u + 4 - i) % 4
-        for j in range(1, 4):
-            from_v = (v + 4 - j) % 4
-            remote(two(from_u, from_v), two(from_u, from_v), gs.at[4 * j + i], gr.at[4 * j + i], b_peers[j]).wait_recv()
-    for copy in g_sends:
-        copy.wait_send()
+    @pl.when(s == 0)
+    def _():
+        merge()
+
+    pass_on()
 
     def hand_on(b, to):
         return remote(eval_out.at[:, cols(b, BLK)], vin.at[:, cols(b, BLK)], vs.at[b], vr.at[b], to)
@@ -445,6 +476,9 @@
     def weights(m, b):
         return merged[m, b // 2, pl.ds((b % 2) * 2, 2)].reshape(BLK, 128)
 
+    for i in range(4):
+        for j in range(1, 4):
+            gather_b(0, i, j).wait_recv()
     total = jnp.zeros((ROWS, 128), F32)
     acc = jnp.zeros((ROWS, 128), F32)
     for b in range(4):
@@ -459,6 +493,9 @@
         acc = acc + dot_nn(vt, weights(0, b))
     sv = lax.rsqrt(jnp.sum(total, axis=1, keepdims=True) * (1.0 / D) + norm_eps)
     av = gelu_value(sv * acc).astype(BF16)
+    for i in range(4):
+        for j in range(1, 4):
+            gather_b(1, i, j).wait_recv()
     for b in range(4):
         eval_out[:, cols(b, BLK)] = (
             vin[:, cols(b, BLK)].astype(F32) + dot_nt(av, weights(1, b))
@@ -472,13 +509,26 @@
         def _(b=b):
             hand_on(b, after).start()
 
+    for m in range(2):
+        flog_out[m] = jnp.log(dens[yl, m])
     for b in range(4):
 
         @pl.when(s != 3)
         def _(b=b):
             hand_on(b, partner).wait_send()
 
+    for m in range(2):
+        for j in range(1, 4):
+            gather_a(m, j).wait_send()
+            for i in range(4):
+                gather_b(m, i, j).wait_send()
     for k in range(4):
+        for q in range(2):
+
+            @pl.when(jnp.logical_not(is_me(k, q)))
+            def _(k=k, q=q):
+                along_y(k, q).wait_send()
+
         give_half(k).wait_send()
         for i in range(1, 4):
             stage_one(k, i, r2.at[k, i - 1]).wait_send()
@@ -524,12 +574,13 @@
             pltpu.VMEM((4, 2, 4, 144, 128), BF16),
             pltpu.VMEM((4, 3, 2, 144, 128), BF16),
             pltpu.VMEM((4, 2, 144, 128), BF16),
-            pltpu.VMEM((4, 2, 144, 128), BF16),
-            pltpu.VMEM((4, 2, 144, 128), BF16),
+            pltpu.VMEM((4, 2, 2, 144, 128), BF16),
+            pltpu.VMEM((2, 2, 144, 128), F32),
+            pltpu.VMEM((4, 2, 2, 144, 128), BF16),
             pltpu.VMEM((2, 2, 4, 4, 144, 128), BF16),
             pltpu.VMEM((ROWS, D), BF16),
             pltpu.VMEM((N, 128), F32),
-            dma((16,)),
+            dma((32,)),
             dma((2,)), dma((2,)),
             dma((2,)), dma((2,)),
             dma((4,)), dma((4,)),
@@ -540,7 +591,8 @@
             dma((4, 4)), dma((4, 4)),
             dma((4, 4)), dma((4, 4)),
             dma((4, 2)), dma((4, 2)),
-            dma((16,)), dma((16,)),
+            dma((2, 4)), dma((2, 4)),
+            dma((2, 4, 4)), dma((2, 4, 4)),
             dma((4,)), dma((4,)),
         ],
         compiler_params=pltpu.CompilerParams(

time: 139 us -> 126 us (0.906)
  Pallas kernels: 130 us -> 118 us
    pallas_call x1, Pallas kernels: 130 us -> 118 us  [local(): pl.pallas_call(kernel, out_shape=(jax.ShapeDtypeStruct((ROWS, D), BF16),...]
where the time goes in v3:
time: 126 us; the launch traced here: 125 us
  Pallas kernels  118 us (94%)
  local copies, waits for them, and re-layouts  6.58 us (5%)
    pallas_call x1, Pallas kernels, local(): pl.pallas_call(kernel, out_shape=(jax.ShapeDtypeStruct((ROWS, D), BF16),...  118 us
    unnamed x3, local copies, waits for them, and re-layouts  3.98 us

profile of v3, /device:TPU:17, one launch (start us, length us, event | category | flops | bytes accessed | tf_op | source)
XLA Modules:
  0.0 125.4 jit_solution(15846093372563992304)
XLA Ops:
  0.6 0.7 copy.10
  1.3 0.1 broadcast_in_dim.13
  1.4 0.9 broadcast_in_dim.14.labels
  2.3 118.2 %merge.1 = (bf16[32,4608]{1,0:T(8,128)(2,1)}, f32[160,128]{1,0:T(8,128)}, f32[2,144,128]{2,1,0:T(8,128)}) custom-call(bf16[4,4608,128]{2,1,0:T(8,128)(2,1)} %bitcast.5, bf16[4,4608,128]{2,1,0:T(8,128)(2,1)} %bitcast.6, bf16[160,4608]{1,0:T(8,128)(2,1)} %bitcast.7, s32[4,160,128]{2,1,0:T(8,128)} %broadcast_in_dim.14.labels, bf16[256,4608]{1,0:T(8,128)(2,1)} %label_rows.1, ...), custom_call_target="tpu_custom_call" | custom-call | tf_op jit(solution)/shard_map/merge/pallas_call | solution.py:551
  120.5 1.0 slice_reduce_fusion
  121.5 0.7 reshape_squeeze.4
  122.1 1.7 %copy.14 = bf16[1,32,4608]{2,1,0:T(8,128)(2,1)} copy(bf16[1,32,4608]{2,1,0:T(8,128)(2,1)} %bitcast.8) | data formatting | bytes 589824
  123.8 1.6 %copy.15 = f32[1,2,144,128]{3,2,1,0:T(8,128)} copy(f32[1,2,144,128]{3,2,1,0:T(8,128)} %bitcast.9) | data formatting | bytes 294912

commit v4 on v3

--- a/solution.py
+++ b/solution.py
@@ -67,7 +67,7 @@
     eval_out, logp_out, flog_out,
     w, x, g, rows, lab, wide, narrow, hid, act, scale,
     fb, r1, r2, s2, r3, s3, r4, dens, wd, merged, vin, picked,
-    load_sem, ps, pr, cs, cr, as_, ar, bs, br, os_, orr, es, er, fs, fr,
+    load_sem, ps, pr, cs, cr, as_, ar, bs, br, bfs, bfr, os_, orr, es, er, fs, fr,
     s1s, s1r, s2s, s2r, ys, yr, gas, gar, gbs, gbr, vs, vr,
 ):
     s = lax.axis_index("section")
@@ -113,15 +113,14 @@
     pl.semaphore_wait(barrier, len(everyone))
 
     far = 3 - y
-    own = u * 4 + v
     part = D // 16
-    slice_rows = pl.ds(own * part, part)
-    cross = [
-        remote(down.at[far, slice_rows], w.at[s, 0, slice_rows], cs.at[0], cr.at[0], across),
-        remote(up.at[far, slice_rows], w.at[s, 1, slice_rows], cs.at[1], cr.at[1], across),
-    ]
-    for copy in cross:
-        copy.start()
+    def cross(t, m):
+        place = pl.ds((((u + 2 * t) % 4) * 4 + v) * part, part)
+        return remote((down, up)[m].at[far, place], w.at[s, m, place], cs.at[t, m], cr.at[t, m], across)
+
+    for t in range(2):
+        for m in range(2):
+            cross(t, m).start()
     beside = [
         remote(down.at[y], w.at[s, 0], ps.at[0], pr.at[0], partner),
         remote(up.at[y], w.at[s, 1], ps.at[1], pr.at[1], partner),
@@ -168,35 +167,52 @@
 
     lr = 2 * (1 - h) + c
 
-    def piece(u_, v_):
-        return w.at[lr, :, pl.ds((u_ * 4 + v_) * part, part)]
-
-    for copy in cross:
-        copy.wait_recv()
-    a_sends = []
-    for i in range(1, 4):
-        copy = remote(piece(u, v), piece(u, v), as_.at[i], ar.at[i], a_peers[i])
-        copy.start()
-        a_sends.append(copy)
-    b_sends = []
-    for i in range(4):
-        if i:
-            from_u = (u + 4 - i) % 4
-            remote(piece(from_u, v), piece(from_u, v), as_.at[i], ar.at[i], a_peers[i]).wait_recv()
-        else:
-            from_u = u
-        for j in range(1, 4):
-            copy = remote(piece(from_u, v), piece(from_u, v), bs.at[i, j], br.at[i, j], b_peers[j])
-            copy.start()
-            b_sends.append(copy)
+    def piece(m, o, e):
+        return w.at[lr, m, pl.ds((((u + o) % 4) * 4 + (v + e) % 4) * part, part)]
+
+    def along_a(m, i):
+        return remote(piece(m, 0, 0), piece(m, 0, 0), as_.at[m, i], ar.at[m, i], a_peers[i])
+
+    def along_b(m, o, j):
+        return remote(piece(m, o, 0), piece(m, o, 0), bs.at[m, o, j], br.at[m, o, j], b_peers[j])
+
+    def further(m, o):
+        view = piece(m, o, 3 if m == 0 else 1)
+        return remote(view, view, bfs.at[m, o], bfr.at[m, o], b_peers[1 if m == 0 else 3])
+
+    def to_b(o, m):
+        along_b(m, o, 1).start()
+        along_b(m, o, 3).start()
+
+    def to_further(o):
+        along_b(0, o, 1).wait_recv()
+        further(0, o).start()
+        along_b(1, o, 3).wait_recv()
+        further(1, o).start()
+
+    for m in range(2):
+        cross(0, m).wait_recv()
+        along_a(m, 1).start()
+        along_a(m, 3).start()
+        to_b(0, m)
+    for m in range(2):
+        for o in (1, 3):
+            along_a(m, 4 - o).wait_recv()
+            to_b(o, m)
+    to_further(0)
+    for m in range(2):
+        cross(1, m).wait_recv()
+        to_b(2, m)
     o_sends = []
-    for i in range(4):
-        from_u = (u + 4 - i) % 4
-        for j in range(1, 4):
-            from_v = (v + 4 - j) % 4
-            remote(piece(from_u, from_v), piece(from_u, from_v), bs.at[i, j], br.at[i, j], b_peers[j]).wait_recv()
-        block = w.at[lr, :, pl.ds(from_u * BLK, BLK)]
-        copy = remote(block, block, os_.at[i], orr.at[i], partner)
+    for o in (1, 3, 2):
+        to_further(o)
+    for o in (0, 1, 3, 2):
+        along_b(0, o, 3).wait_recv()
+        along_b(1, o, 1).wait_recv()
+        for m in range(2):
+            further(m, o).wait_recv()
+        view = w.at[lr, :, pl.ds(((u + o) % 4) * BLK, BLK)]
+        copy = remote(view, view, os_.at[o], orr.at[o], partner)
         copy.start()
         o_sends.append(copy)
 
@@ -214,8 +230,15 @@
         copy.wait()
     for copy in loads:
         copy.wait()
-    for copy in cross + a_sends + b_sends:
-        copy.wait_send()
+    for m in range(2):
+        for t in range(2):
+            cross(t, m).wait_send()
+        for j in (1, 3):
+            along_a(m, j).wait_send()
+            for o in range(4):
+                along_b(m, o, j).wait_send()
+        for o in range(4):
+            further(m, o).wait_send()
     for copy in o_sends:
         copy.wait()
 
@@ -258,9 +281,12 @@
     bent = jnp.tanh(logits * (1.0 / soft_cap))
     capped = soft_cap * bent
     logp = capped - jnp.log(jnp.sum(jnp.exp(capped), axis=1, keepdims=True))
-    hot = lab[:, 0:1] == lax.broadcasted_iota(jnp.int32, (N, LABELS), 1)
-    chosen = jnp.sum(jnp.where(hot, logp, 0.0), axis=1, keepdims=True)
-    picked[...] = jnp.broadcast_to(chosen, (N, 128))
+    word = lax.broadcasted_iota(jnp.int32, (LABELS, ROWS), 0)
+    marks = [jnp.where(word == lab[m : m + 1, :], 1.0, 0.0) for m in range(MICRO)]
+    hot = jnp.concatenate([jnp.transpose(mark) for mark in marks], axis=0)
+    for m in range(MICRO):
+        part_logp = jnp.transpose(logp[m * ROWS : (m + 1) * ROWS, :])
+        picked[m : m + 1, :] = jnp.sum(part_logp * marks[m], axis=0, keepdims=True)
     give = remote(picked, logp_out, es.at[2], er.at[2], swap)
     hold = pltpu.make_async_copy(picked, logp_out, load_sem.at[14])
 
@@ -272,7 +298,7 @@
     def _():
         hold.start()
 
-    e = ((jnp.exp(logp) - jnp.where(hot, 1.0, 0.0)) * (1.0 - bent * bent)).astype(BF16)
+    e = ((jnp.exp(logp) - hot) * (1.0 - bent * bent)).astype(BF16)
     mean = jnp.sum(e.astype(F32) * logits, axis=1, keepdims=True) * (1.0 / D)
     sm = sy * mean
 
@@ -372,11 +398,19 @@
         peers = (x_peers, z_peers)[m]
         return remote(block(m, xx, zz), block(m, xx, zz), gas.at[m, i], gar.at[m, i], peers[i])
 
+    def gathered(m, i, e):
+        x_ = (xx + 4 - i) % 4 if m == 0 else (xx + e) % 4
+        z_ = (zz + 4 - i) % 4 if m == 1 else (zz + e) % 4
+        return x_, z_
+
     def gather_b(m, i, j):
-        x_ = (xx + 4 - i) % 4 if m == 0 else xx
-        z_ = (zz + 4 - i) % 4 if m == 1 else zz
-        peers = (z_peers, x_peers)[m]
-        return remote(block(m, x_, z_), block(m, x_, z_), gbs.at[m, i, j], gbr.at[m, i, j], peers[j])
+        view = block(m, *gathered(m, i, 0))
+        return remote(view, view, gbs.at[m, i, j], gbr.at[m, i, j], (z_peers, x_peers)[m][j])
+
+    def gather_on(m, i, a):
+        view = merged.at[(m, a, *gathered(m, i, 3 if a == 0 else 1))]
+        to = (z_peers, x_peers)[m][1 if a == 0 else 3]
+        return remote(view, view, gbs.at[m, i, 2 * a], gbr.at[m, i, 2 * a], to)
 
     def merge():
         for i in range(4):
@@ -406,12 +440,28 @@
                 gather_a(m, i).start()
 
     def pass_on():
-        for i in (0, 1, 3, 2):
+        def onward(m, i):
+            gather_b(m, i, 1).wait_recv()
+            gather_on(m, i, 0).start()
+            gather_b(m, i, 3).wait_recv()
+            gather_on(m, i, 1).start()
+
+        def direct(m, i):
+            if i:
+                gather_a(m, i).wait_recv()
+            gather_b(m, i, 1).start()
+            gather_b(m, i, 3).start()
+
+        for i in (0, 1, 3):
             for m in range(2):
-                if i:
-                    gather_a(m, i).wait_recv()
-                for j in (1, 3, 2):
-                    gather_b(m, i, j).start()
+                direct(m, i)
+        for m in range(2):
+            onward(m, 0)
+        for m in range(2):
+            direct(m, 2)
+        for i in (1, 3, 2):
+            for m in range(2):
+                onward(m, i)
 
     for k in (3, 2, 1, 0):
         hk = hid[k]
@@ -477,8 +527,8 @@
         return merged[m, b // 2, pl.ds((b % 2) * 2, 2)].reshape(BLK, 128)
 
     for i in range(4):
-        for j in range(1, 4):
-            gather_b(0, i, j).wait_recv()
+        for a in range(2):
+            gather_on(0, i, a).wait_recv()
     total = jnp.zeros((ROWS, 128), F32)
     acc = jnp.zeros((ROWS, 128), F32)
     for b in range(4):
@@ -494,8 +544,8 @@
     sv = lax.rsqrt(jnp.sum(total, axis=1, keepdims=True) * (1.0 / D) + norm_eps)
     av = gelu_value(sv * acc).astype(BF16)
     for i in range(4):
-        for j in range(1, 4):
-            gather_b(1, i, j).wait_recv()
+        for a in range(2):
+            gather_on(1, i, a).wait_recv()
     for b in range(4):
         eval_out[:, cols(b, BLK)] = (
             vin[:, cols(b, BLK)].astype(F32) + dot_nt(av, weights(1, b))
@@ -520,8 +570,11 @@
     for m in range(2):
         for j in range(1, 4):
             gather_a(m, j).wait_send()
-            for i in range(4):
+        for i in range(4):
+            for j in (1, 3):
                 gather_b(m, i, j).wait_send()
+            for a in range(2):
+                gather_on(m, i, a).wait_send()
     for k in range(4):
         for q in range(2):
 
@@ -547,12 +600,11 @@
     vmem = pl.BlockSpec(memory_space=pltpu.VMEM)
     hbm = pl.BlockSpec(memory_space=pl.ANY)
     dma = pltpu.SemaphoreType.DMA
-    labels = jnp.broadcast_to(sampled_labels.reshape(TASKS, N, 1), (TASKS, N, 128))
     eval_out, logp, flog = pl.pallas_call(
         kernel,
         out_shape=(
             jax.ShapeDtypeStruct((ROWS, D), BF16),
-            jax.ShapeDtypeStruct((N, 128), F32),
+            jax.ShapeDtypeStruct((MICRO, ROWS), F32),
             jax.ShapeDtypeStruct((2, 144, 128), F32),
         ),
         in_specs=[hbm] * 6,
@@ -562,7 +614,7 @@
             pltpu.VMEM((5, N, D), BF16),
             pltpu.VMEM((N, D), BF16),
             pltpu.VMEM((LABELS, D), BF16),
-            pltpu.VMEM((N, 128), jnp.int32),
+            pltpu.VMEM((MICRO, ROWS), jnp.int32),
             pltpu.VMEM((2, N, D), BF16),
             pltpu.VMEM((2, N, R), BF16),
             pltpu.VMEM((4, N, R), F32),
@@ -579,12 +631,13 @@
             pltpu.VMEM((4, 2, 2, 144, 128), BF16),
             pltpu.VMEM((2, 2, 4, 4, 144, 128), BF16),
             pltpu.VMEM((ROWS, D), BF16),
-            pltpu.VMEM((N, 128), F32),
+            pltpu.VMEM((MICRO, ROWS), F32),
             dma((32,)),
             dma((2,)), dma((2,)),
-            dma((2,)), dma((2,)),
-            dma((4,)), dma((4,)),
-            dma((4, 4)), dma((4, 4)),
+            dma((2, 2)), dma((2, 2)),
+            dma((2, 4)), dma((2, 4)),
+            dma((2, 4, 4)), dma((2, 4, 4)),
+            dma((2, 4)), dma((2, 4)),
             dma((4,)), dma((4,)),
             dma((3,)), dma((3,)),
             dma((4,)), dma((4,)),
@@ -603,13 +656,13 @@
         down_proj.reshape(TASKS, D, R),
         up_proj.reshape(TASKS, D, R),
         entry_states.reshape(N, D),
-        labels,
+        sampled_labels,
         label_rows,
         eval_states,
     )
     return (
         eval_out[None],
-        logp[:, 0].reshape(1, MICRO, ROWS),
+        logp[None],
         flog[None],
     )
 

time: 126 us -> 122 us (0.968)
  Pallas kernels: 118 us -> 115 us
    pallas_call x1, Pallas kernels: 118 us -> 115 us  [local(): pl.pallas_call(kernel, out_shape=(jax.ShapeDtypeStruct((ROWS, D), BF16),...]
    unnamed x3 -> x4, local copies, waits for them, and re-layouts: 3.98 us -> 5.84 us
where the time goes in v4:
time: 122 us
  Pallas kernels  115 us (94%)
  local copies, waits for them, and re-layouts  5.84 us (5%)
    pallas_call x1, Pallas kernels, local(): pl.pallas_call(kernel, out_shape=(jax.ShapeDtypeStruct((ROWS, D), BF16),...  115 us
    unnamed x4, local copies, waits for them, and re-layouts  5.84 us

profile of v4, /device:TPU:17, one launch (start us, length us, event | category | flops | bytes accessed | tf_op | source)
XLA Modules:
  0.0 121.6 jit_solution(9072888235098840960)
XLA Ops:
  0.6 1.3 %copy.9.labels = s32[4,5,32]{2,1,0:T(8,128)} copy(s32[4,5,32]{2,0,1:T(4,128)} %param.10) | data formatting | bytes 5120 | tf_op args[4]
  1.9 115.1 %merge.1 = (bf16[32,4608]{1,0:T(8,128)(2,1)}, f32[5,32]{1,0:T(8,128)}, f32[2,144,128]{2,1,0:T(8,128)}) custom-call(bf16[4,4608,128]{2,1,0:T(8,128)(2,1)} %bitcast.6, bf16[4,4608,128]{2,1,0:T(8,128)(2,1)} %bitcast.7, bf16[160,4608]{1,0:T(8,128)(2,1)} %bitcast.8, s32[4,5,32]{2,1,0:T(8,128)} %copy.9.labels, bf16[256,4608]{1,0:T(8,128)(2,1)} %label_rows.1, ...), custom_call_target="tpu_custom_call" | custom-call | tf_op jit(solution)/shard_map/merge/pallas_call | solution.py:603
  117.0 1.3 %copy.10 = f32[1,5,32]{2,0,1:T(1,128)} copy(f32[1,5,32]{2,1,0:T(8,128)} %bitcast.11) | data formatting | bytes 1280
  118.3 1.7 %copy.13 = bf16[1,32,4608]{2,1,0:T(8,128)(2,1)} copy(bf16[1,32,4608]{2,1,0:T(8,128)(2,1)} %bitcast.9) | data formatting | bytes 589824
  120.0 1.6 %copy.14 = f32[1,2,144,128]{3,2,1,0:T(8,128)} copy(f32[1,2,144,128]{3,2,1,0:T(8,128)} %bitcast.10) | data formatting | bytes 294912

commit v5 on v4

--- a/solution.py
+++ b/solution.py
@@ -118,9 +118,8 @@
         place = pl.ds((((u + 2 * t) % 4) * 4 + v) * part, part)
         return remote((down, up)[m].at[far, place], w.at[s, m, place], cs.at[t, m], cr.at[t, m], across)
 
-    for t in range(2):
-        for m in range(2):
-            cross(t, m).start()
+    for m in range(2):
+        cross(0, m).start()
     beside = [
         remote(down.at[y], w.at[s, 0], ps.at[0], pr.at[0], partner),
         remote(up.at[y], w.at[s, 1], ps.at[1], pr.at[1], partner),
@@ -192,6 +191,7 @@
 
     for m in range(2):
         cross(0, m).wait_recv()
+        cross(1, m).start()
         along_a(m, 1).start()
         along_a(m, 3).start()
         to_b(0, m)
@@ -320,8 +320,19 @@
     def give_half(k):
         return remote(fb.at[k, 1 - c], r1.at[k], fs.at[k], fr.at[k], partner)
 
+    up_one, down_one = (u + 1) % 4, (u + 3) % 4
+
     def stage_one(k, i, view):
-        return remote(view, r2.at[k, i - 1], s1s.at[k, i], s1r.at[k, i], a_peers[i])
+        return remote(view, r2.at[k, i], s1s.at[k, i], s1r.at[k, i], a_peers[1 if i in (0, 1, 4) else 3])
+
+    def with_block(k, body):
+        @pl.when(c == 0)
+        def _():
+            body(lambda t, a: fb.at[k, 0, a, t])
+
+        @pl.when(c == 1)
+        def _():
+            body(lambda t, a: fb.at[k, 1, a, :, t])
 
     def open_sum(k):
         remote(fb.at[k, c], r1.at[k], fs.at[k], fr.at[k], partner).wait_recv()
@@ -329,39 +340,49 @@
             for b in range(4):
                 fb[k, c, a, b] = (fb[k, c, a, b].astype(F32) + r1[k, a, b].astype(F32)).astype(BF16)
 
-        @pl.when(c == 0)
-        def _():
-            for i in (2, 1, 3):
-                stage_one(k, i, fb.at[k, 0, :, (u + i) % 4]).start()
-
-        @pl.when(c == 1)
-        def _():
-            for i in (2, 1, 3):
-                stage_one(k, i, fb.at[k, 1, :, :, (u + i) % 4]).start()
+        def send(view):
+            stage_one(k, 4, view((u + 2) % 4, 0)).start()
+            stage_one(k, 5, view((u + 2) % 4, 1)).start()
+
+        with_block(k, send)
+
+    def direct_sum(k):
+        def send(view):
+            stage_one(k, 1, view(up_one, 1)).start()
+            stage_one(k, 3, view(down_one, 0)).start()
+
+        with_block(k, send)
+
+    def relay_sum(k):
+        for i in (4, 5):
+            stage_one(k, i, r2.at[k, i]).wait_recv()
+
+        def send(view):
+            for i, t, a in ((4, up_one, 0), (5, down_one, 1)):
+                own_part = view(t, a)
+                for b in range(4):
+                    r2[k, i, b] = (r2[k, i, b].astype(F32) + own_part[b].astype(F32)).astype(BF16)
+                stage_one(k, 0 if i == 4 else 2, r2.at[k, i]).start()
+
+        with_block(k, send)
 
     def stage_two(k, i):
         return remote(s2.at[k, :, (v + i) % 4], r3.at[k, i - 1], s2s.at[k, i], s2r.at[k, i], b_peers[i])
 
     def middle_sum(k):
-        for i in range(1, 4):
-            stage_one(k, i, r2.at[k, i - 1]).wait_recv()
-
-        def add_with(load):
-            for a in range(2):
+        for i in range(4):
+            stage_one(k, i, r2.at[k, i]).wait_recv()
+
+        def add(view):
+            for a, pair in ((0, (0, 3)), (1, (1, 2))):
+                own_part = view(u, a)
                 for b in range(4):
-                    value = load(a, b).astype(F32)
-                    for i in range(3):
-                        value = value + r2[k, i, a, b].astype(F32)
+                    value = own_part[b].astype(F32)
+                    for i in pair:
+                        value = value + r2[k, i, b].astype(F32)
                     s2[k, a, b] = value.astype(BF16)
 
-        @pl.when(c == 0)
-        def _():
-            add_with(lambda a, b: fb[k, 0, a, u, b])
-
-        @pl.when(c == 1)
-        def _():
-            add_with(lambda a, b: fb[k, 1, a, b, u])
-
+        with_block(k, add)
         for i in (2, 1, 3):
             stage_two(k, i).start()
 
@@ -493,16 +514,29 @@
             return acc + dot_nn(gy, w[k - 1, 1, cols(f), :])
 
         ga = over(D // TILE, step, zero)
-        open_sum(k)
+        if k == 3:
+            open_sum(3)
+            direct_sum(3)
+        if k == 2:
+            relay_sum(3)
+            open_sum(2)
+            direct_sum(2)
+        if k == 1:
+            relay_sum(2)
+            open_sum(1)
+            direct_sum(1)
 
     middle_sum(3)
     open_sum(0)
+    relay_sum(1)
+    relay_sum(0)
+    direct_sum(0)
+    middle_sum(2)
     last_sum(3)
-    middle_sum(2)
+    middle_sum(1)
+    middle_sum(0)
     last_sum(2)
-    middle_sum(1)
     last_sum(1)
-    middle_sum(0)
 
     @pl.when(s != 0)
     def _():
@@ -583,8 +617,9 @@
                 along_y(k, q).wait_send()
 
         give_half(k).wait_send()
+        for i in range(6):
+            stage_one(k, i, r2.at[k, i]).wait_send()
         for i in range(1, 4):
-            stage_one(k, i, r2.at[k, i - 1]).wait_send()
             stage_two(k, i).wait_send()
 
     @pl.when(c != yl)
@@ -594,6 +629,17 @@
     @pl.when(c == yl)
     def _():
         hold.wait()
+
+
+def settle(eval_in, logp_in, flog_in, eval_out, logp_out, flog_out, ev, lo, fl, sem_in, sem_out):
+    takes = [(eval_in, ev, eval_out), (logp_in, lo, logp_out), (flog_in, fl, flog_out)]
+    for i, (source, held, _) in enumerate(takes):
+        pltpu.make_async_copy(source, held, sem_in.at[i]).start()
+    for i, (source, held, target) in enumerate(takes):
+        pltpu.make_async_copy(source, held, sem_in.at[i]).wait()
+        pltpu.make_async_copy(held, target, sem_out.at[i]).start()
+    for i, (_, held, target) in enumerate(takes):
+        pltpu.make_async_copy(held, target, sem_out.at[i]).wait()
 
 
 def local(entry_states, down_proj, up_proj, label_rows, sampled_labels, eval_states):
@@ -622,7 +668,7 @@
             pltpu.VMEM((4, N, 128), F32),
             pltpu.VMEM((4, 2, 2, 4, 4, 144, 128), BF16),
             pltpu.VMEM((4, 2, 4, 4, 144, 128), BF16),
-            pltpu.VMEM((4, 3, 2, 4, 144, 128), BF16),
+            pltpu.VMEM((4, 6, 4, 144, 128), BF16),
             pltpu.VMEM((4, 2, 4, 144, 128), BF16),
             pltpu.VMEM((4, 3, 2, 144, 128), BF16),
             pltpu.VMEM((4, 2, 144, 128), BF16),
@@ -641,7 +687,7 @@
             dma((4,)), dma((4,)),
             dma((3,)), dma((3,)),
             dma((4,)), dma((4,)),
-            dma((4, 4)), dma((4, 4)),
+            dma((4, 6)), dma((4, 6)),
             dma((4, 4)), dma((4, 4)),
             dma((4, 2)), dma((4, 2)),
             dma((2, 4)), dma((2, 4)),
@@ -660,6 +706,20 @@
         label_rows,
         eval_states,
     )
+    eval_out, logp, flog = pl.pallas_call(
+        settle,
+        out_shape=tuple(jax.ShapeDtypeStruct(o.shape, o.dtype) for o in (eval_out, logp, flog)),
+        in_specs=[hbm] * 3,
+        out_specs=(hbm, hbm, hbm),
+        scratch_shapes=[
+            pltpu.VMEM((ROWS, D), BF16),
+            pltpu.VMEM((MICRO, ROWS), F32),
+            pltpu.VMEM((2, 144, 128), F32),
+            dma((3,)),
+            dma((3,)),
+        ],
+        name="settle",
+    )(eval_out, logp, flog)
     return (
         eval_out[None],
         logp[None],

time: 122 us -> 119 us (0.975)
  local copies, waits for them, and re-layouts: 5.84 us -> 2.57 us
    unnamed x4 -> x2, local copies, waits for them, and re-layouts: 5.84 us -> 2.57 us
    pallas_call x0 -> x1, Pallas kernels: none -> 1.78 us  [local(): pl.pallas_call(settle, out_shape=tuple((jax.ShapeDtypeStruct(o.shape, o.d...]
    pallas_call x1, Pallas kernels: 115 us -> 114 us  [local(): pl.pallas_call(kernel, out_shape=(jax.ShapeDtypeStruct((ROWS, D), BF16),...]
where the time goes in v5:
time: 119 us
  Pallas kernels  115 us (97%)
  local copies, waits for them, and re-layouts  2.57 us (2%)
    pallas_call x1, Pallas kernels, local(): pl.pallas_call(kernel, out_shape=(jax.ShapeDtypeStruct((ROWS, D), BF16),...  114 us
    unnamed x2, local copies, waits for them, and re-layouts  2.57 us

profile of v5, /device:TPU:17, one launch (start us, length us, event | category | flops | bytes accessed | tf_op | source)
XLA Modules:
  0.0 118.6 jit_solution(12957862467151146815)
XLA Ops:
  0.6 1.3 %copy.9.labels = s32[4,5,32]{2,1,0:T(8,128)} copy(s32[4,5,32]{2,0,1:T(4,128)} %param.10) | data formatting | bytes 5120 | tf_op args[4]
  1.9 113.6 %merge.1 = (bf16[32,4608]{1,0:T(8,128)(2,1)}, f32[5,32]{1,0:T(8,128)}, f32[2,144,128]{2,1,0:T(8,128)}) custom-call(bf16[4,4608,128]{2,1,0:T(8,128)(2,1)} %bitcast.6, bf16[4,4608,128]{2,1,0:T(8,128)(2,1)} %bitcast.7, bf16[160,4608]{1,0:T(8,128)(2,1)} %bitcast.8, s32[4,5,32]{2,1,0:T(8,128)} %copy.9.labels, bf16[256,4608]{1,0:T(8,128)(2,1)} %label_rows.1, ...), custom_call_target="tpu_custom_call" | custom-call | tf_op jit(solution)/shard_map/merge/pallas_call | solution.py:649
  115.5 1.8 %settle.1 = (bf16[32,4608]{1,0:T(8,128)(2,1)}, f32[5,32]{1,0:T(8,128)}, f32[2,144,128]{2,1,0:T(8,128)}) custom-call(bf16[32,4608]{1,0:T(8,128)(2,1)} %get-tuple-element.9.eval_in, f32[5,32]{1,0:T(8,128)} %get-tuple-element.10.logp_in, f32[2,144,128]{2,1,0:T(8,128)} %get-tuple-element.11.flog_in), custom_call_target="tpu_custom_call" | custom-call | tf_op jit(solution)/shard_map/settle/pallas_call | solution.py:709
  117.3 1.3 %copy.10 = f32[1,5,32]{2,0,1:T(1,128)} copy(f32[1,5,32]{2,1,0:T(8,128)} %bitcast.9) | data formatting | bytes 1280

commit v6 on v5

--- a/solution.py
+++ b/solution.py
@@ -126,11 +126,11 @@
     ]
     moved = [
         remote(entry, x.at[0], es.at[0], er.at[0], swap),
-        remote(labels.at[2 * h + 1 - yl], lab, es.at[1], er.at[1], swap),
+        remote(labels, lab, es.at[1], er.at[1], swap),
     ]
     kept = [
         pltpu.make_async_copy(entry, x.at[0], load_sem.at[0]),
-        pltpu.make_async_copy(labels.at[y], lab, load_sem.at[1]),
+        pltpu.make_async_copy(labels, lab, load_sem.at[1]),
     ]
 
     @pl.when(c != yl)
@@ -282,11 +282,11 @@
     capped = soft_cap * bent
     logp = capped - jnp.log(jnp.sum(jnp.exp(capped), axis=1, keepdims=True))
     word = lax.broadcasted_iota(jnp.int32, (LABELS, ROWS), 0)
-    marks = [jnp.where(word == lab[m : m + 1, :], 1.0, 0.0) for m in range(MICRO)]
+    marks = [jnp.where(word == lab[m, pl.ds(y, 1), :], 1.0, 0.0) for m in range(MICRO)]
     hot = jnp.concatenate([jnp.transpose(mark) for mark in marks], axis=0)
     for m in range(MICRO):
         part_logp = jnp.transpose(logp[m * ROWS : (m + 1) * ROWS, :])
-        picked[m : m + 1, :] = jnp.sum(part_logp * marks[m], axis=0, keepdims=True)
+        picked[m] = jnp.sum(part_logp * marks[m], axis=0, keepdims=True)
     give = remote(picked, logp_out, es.at[2], er.at[2], swap)
     hold = pltpu.make_async_copy(picked, logp_out, load_sem.at[14])
 
@@ -317,8 +317,8 @@
 
     ga = over(D // TILE, head, zero)
 
-    def give_half(k):
-        return remote(fb.at[k, 1 - c], r1.at[k], fs.at[k], fr.at[k], partner)
+    def give_half(k, m):
+        return remote(fb.at[k, m], r1.at[k], fs.at[k], fr.at[k], partner)
 
     up_one, down_one = (u + 1) % 4, (u + 3) % 4
 
@@ -335,7 +335,7 @@
             body(lambda t, a: fb.at[k, 1, a, :, t])
 
     def open_sum(k):
-        remote(fb.at[k, c], r1.at[k], fs.at[k], fr.at[k], partner).wait_recv()
+        give_half(k, c).wait_recv()
         for a in range(2):
             for b in range(4):
                 fb[k, c, a, b] = (fb[k, c, a, b].astype(F32) + r1[k, a, b].astype(F32)).astype(BF16)
@@ -500,7 +500,7 @@
                 value = dot_tn(wide[m, :, cols(b, BLK)], thin).astype(BF16)
                 fb[k, m, b // 2, pl.ds((b % 2) * 2, 2)] = value.reshape(2, 4, 144, 128)
             if m is not c:
-                give_half(k).start()
+                give_half(k, m).start()
         if k == 0:
             break
 
@@ -522,29 +522,34 @@
             open_sum(2)
             direct_sum(2)
         if k == 1:
+            middle_sum(3)
             relay_sum(2)
             open_sum(1)
             direct_sum(1)
 
-    middle_sum(3)
     open_sum(0)
     relay_sum(1)
+    direct_sum(0)
     relay_sum(0)
-    direct_sum(0)
     middle_sum(2)
+    middle_sum(1)
     last_sum(3)
-    middle_sum(1)
+    last_sum(1)
     middle_sum(0)
+
+    @pl.when(c == 1)
+    def _():
+        merge()
+
     last_sum(2)
-    last_sum(1)
-
-    @pl.when(s != 0)
+    last_sum(0)
+
+    @pl.when(s == 0)
     def _():
         merge()
 
-    last_sum(0)
-
-    @pl.when(s == 0)
+
+    @pl.when(s == 2)
     def _():
         merge()
 
@@ -616,7 +621,7 @@
             def _(k=k, q=q):
                 along_y(k, q).wait_send()
 
-        give_half(k).wait_send()
+        give_half(k, 1 - c).wait_send()
         for i in range(6):
             stage_one(k, i, r2.at[k, i]).wait_send()
         for i in range(1, 4):
@@ -650,7 +655,7 @@
         kernel,
         out_shape=(
             jax.ShapeDtypeStruct((ROWS, D), BF16),
-            jax.ShapeDtypeStruct((MICRO, ROWS), F32),
+            jax.ShapeDtypeStruct((MICRO, 1, ROWS), F32),
             jax.ShapeDtypeStruct((2, 144, 128), F32),
         ),
         in_specs=[hbm] * 6,
@@ -660,7 +665,7 @@
             pltpu.VMEM((5, N, D), BF16),
             pltpu.VMEM((N, D), BF16),
             pltpu.VMEM((LABELS, D), BF16),
-            pltpu.VMEM((MICRO, ROWS), jnp.int32),
+            pltpu.VMEM((MICRO, TASKS, ROWS), jnp.int32),
             pltpu.VMEM((2, N, D), BF16),
             pltpu.VMEM((2, N, R), BF16),
             pltpu.VMEM((4, N, R), F32),
@@ -677,7 +682,7 @@
             pltpu.VMEM((4, 2, 2, 144, 128), BF16),
             pltpu.VMEM((2, 2, 4, 4, 144, 128), BF16),
             pltpu.VMEM((ROWS, D), BF16),
-            pltpu.VMEM((MICRO, ROWS), F32),
+            pltpu.VMEM((MICRO, 1, ROWS), F32),
             dma((32,)),
             dma((2,)), dma((2,)),
             dma((2, 2)), dma((2, 2)),
@@ -702,7 +707,7 @@
         down_proj.reshape(TASKS, D, R),
         up_proj.reshape(TASKS, D, R),
         entry_states.reshape(N, D),
-        sampled_labels,
+        jnp.transpose(sampled_labels, (1, 0, 2)),
         label_rows,
         eval_states,
     )
@@ -713,7 +718,7 @@
         out_specs=(hbm, hbm, hbm),
         scratch_shapes=[
             pltpu.VMEM((ROWS, D), BF16),
-            pltpu.VMEM((MICRO, ROWS), F32),
+            pltpu.VMEM((MICRO, 1, ROWS), F32),
             pltpu.VMEM((2, 144, 128), F32),
             dma((3,)),
             dma((3,)),
@@ -722,7 +727,7 @@
     )(eval_out, logp, flog)
     return (
         eval_out[None],
-        logp[None],
+        jnp.transpose(logp, (1, 0, 2)),
         flog[None],
     )
 

time: 119 us -> 115 us (0.966)
  local copies, waits for them, and re-layouts: 2.57 us -> 0 us
    unnamed x2 -> x0, local copies, waits for them, and re-layouts: 2.57 us -> none
    pallas_call x1, Pallas kernels: 114 us -> 112 us  [local(): pl.pallas_call(kernel, out_shape=(jax.ShapeDtypeStruct((ROWS, D), BF16),...]
where the time goes in v6:
time: 115 us
  Pallas kernels  114 us (99%)
    pallas_call x1, Pallas kernels, local(): pl.pallas_call(kernel, out_shape=(jax.ShapeDtypeStruct((ROWS, D), BF16),...  112 us

profile of v6, /device:TPU:17, one launch (start us, length us, event | category | flops | bytes accessed | tf_op | source)
XLA Modules:
  0.0 114.8 jit_solution(4520020708441836732)
XLA Ops:
  0.6 112.2 %merge.1 = (bf16[32,4608]{1,0:T(8,128)(2,1)}, f32[5,1,32]{2,1,0:T(1,128)}, f32[2,144,128]{2,1,0:T(8,128)}) custom-call(bf16[4,4608,128]{2,1,0:T(8,128)(2,1)} %bitcast.7, bf16[4,4608,128]{2,1,0:T(8,128)(2,1)} %bitcast.8, bf16[160,4608]{1,0:T(8,128)(2,1)} %bitcast.9, s32[5,4,32]{2,1,0:T(4,128)} %bitcast.10, bf16[256,4608]{1,0:T(8,128)(2,1)} %label_rows.1, ...), custom_call_target="tpu_custom_call" | custom-call | tf_op jit(solution)/shard_map/merge/pallas_call | solution.py:654
  112.8 1.8 %settle.1 = (bf16[32,4608]{1,0:T(8,128)(2,1)}, f32[5,1,32]{2,1,0:T(1,128)}, f32[2,144,128]{2,1,0:T(8,128)}) custom-call(bf16[32,4608]{1,0:T(8,128)(2,1)} %get-tuple-element.9.eval_in, f32[5,1,32]{2,1,0:T(1,128)} %get-tuple-element.10.logp_in, f32[2,144,128]{2,1,0:T(8,128)} %get-tuple-element.11.flog_in), custom_call_target="tpu_custom_call" | custom-call | tf_op jit(solution)/shard_map/settle/pallas_call | solution.py:714

commit v7 on v6

--- a/solution.py
+++ b/solution.py
@@ -17,7 +17,7 @@
 MICRO = 5
 ROWS = 32
 N = MICRO * ROWS
-TILE = 512
+TILE = 256
 BLK = D // 4
 F32 = jnp.float32
 BF16 = jnp.bfloat16
@@ -636,17 +636,6 @@
         hold.wait()
 
 
-def settle(eval_in, logp_in, flog_in, eval_out, logp_out, flog_out, ev, lo, fl, sem_in, sem_out):
-    takes = [(eval_in, ev, eval_out), (logp_in, lo, logp_out), (flog_in, fl, flog_out)]
-    for i, (source, held, _) in enumerate(takes):
-        pltpu.make_async_copy(source, held, sem_in.at[i]).start()
-    for i, (source, held, target) in enumerate(takes):
-        pltpu.make_async_copy(source, held, sem_in.at[i]).wait()
-        pltpu.make_async_copy(held, target, sem_out.at[i]).start()
-    for i, (_, held, target) in enumerate(takes):
-        pltpu.make_async_copy(held, target, sem_out.at[i]).wait()
-
-
 def local(entry_states, down_proj, up_proj, label_rows, sampled_labels, eval_states):
     vmem = pl.BlockSpec(memory_space=pltpu.VMEM)
     hbm = pl.BlockSpec(memory_space=pl.ANY)
@@ -654,9 +643,9 @@
     eval_out, logp, flog = pl.pallas_call(
         kernel,
         out_shape=(
-            jax.ShapeDtypeStruct((ROWS, D), BF16),
-            jax.ShapeDtypeStruct((MICRO, 1, ROWS), F32),
-            jax.ShapeDtypeStruct((2, 144, 128), F32),
+            pltpu.VMEM((ROWS, D), BF16),
+            pltpu.VMEM((MICRO, 1, ROWS), F32),
+            pltpu.VMEM((2, 144, 128), F32),
         ),
         in_specs=[hbm] * 6,
         out_specs=(vmem, vmem, vmem),
@@ -700,7 +689,7 @@
             dma((4,)), dma((4,)),
         ],
         compiler_params=pltpu.CompilerParams(
-            collective_id=0, has_side_effects=True, vmem_limit_bytes=67043328
+            collective_id=0, has_side_effects=True, vmem_limit_bytes=60000000
         ),
         name="merge",
     )(
@@ -711,20 +700,6 @@
         label_rows,
         eval_states,
     )
-    eval_out, logp, flog = pl.pallas_call(
-        settle,
-        out_shape=tuple(jax.ShapeDtypeStruct(o.shape, o.dtype) for o in (eval_out, logp, flog)),
-        in_specs=[hbm] * 3,
-        out_specs=(hbm, hbm, hbm),
-        scratch_shapes=[
-            pltpu.VMEM((ROWS, D), BF16),
-            pltpu.VMEM((MICRO, 1, ROWS), F32),
-            pltpu.VMEM((2, 144, 128), F32),
-            dma((3,)),
-            dma((3,)),
-        ],
-        name="settle",
-    )(eval_out, logp, flog)
     return (
         eval_out[None],
         jnp.transpose(logp, (1, 0, 2)),

time: 115 us -> 112 us (0.974)
  Pallas kernels: 114 us -> 109 us
  local copies, waits for them, and re-layouts: 0 us -> 1.95 us
    pallas_call x2 -> x1, Pallas kernels: 114 us -> 109 us  [local(): pl.pallas_call(kernel, out_shape=(pltpu.VMEM((ROWS, D), BF16), pltpu.VMEM...]
    unnamed x0 -> x3, local copies, waits for them, and re-layouts: none -> 1.95 us
where the time goes in v7:
time: 112 us; the launch traced here: 111 us
  Pallas kernels  109 us (97%)
  local copies, waits for them, and re-layouts  1.95 us (2%)
    pallas_call x1, Pallas kernels, local(): pl.pallas_call(kernel, out_shape=(pltpu.VMEM((ROWS, D), BF16), pltpu.VMEM...  109 us

profile of v7, /device:TPU:17, one launch (start us, length us, event | category | flops | bytes accessed | tf_op | source)
XLA Modules:
  0.0 111.1 jit_solution(198557312585559043)
XLA Ops:
  0.6 108.5 %merge.1 = (bf16[32,4608]{1,0:T(8,128)(2,1)S(1)}, f32[5,1,32]{2,1,0:T(1,128)S(1)}, f32[2,144,128]{2,1,0:T(8,128)S(1)}) custom-call(bf16[4,4608,128]{2,1,0:T(8,128)(2,1)} %bitcast.10, bf16[4,4608,128]{2,1,0:T(8,128)(2,1)} %bitcast.11, bf16[160,4608]{1,0:T(8,128)(2,1)} %bitcast.12, s32[5,4,32]{2,1,0:T(4,128)} %bitcast.13, bf16[256,4608]{1,0:T(8,128)(2,1)} %label_rows.1, ...), custom_call_target="tpu_custom_call" | custom-call | tf_op jit(solution)/shard_map/merge/pallas_call | solution.py:643
  109.2 0.7 copy.12
  109.9 0.6 copy.13
  110.5 0.7 copy.14
